TPU v7x, 32 devices: a whole 2x2x4 slice. The times are simulated.
32 devices in a mesh: groups: 2 (over x), seq: 16 (over z, y, core).
Axes of the slice: x: 2, y: 2, z: 4, core: 2. Of those that a mesh axis runs over, the one named last changes fastest.
Arguments:
- hidden: bfloat16 [64, 16384], P('groups', 'seq'), parts along dimension 0, may hold values from -6 to 6
- w_query: bfloat16 [16384, 8192], P('seq'), may hold values from -0.046875 to 0.046875
- w_key: bfloat16 [16384, 512], P('seq'), may hold values from -0.25 to 0.25
- w_value: bfloat16 [16384, 512], P('seq'), may hold values from -0.1875 to 0.1875
- w_out: bfloat16 [8192, 16384], P(None, 'seq'), may hold values from -0.0625 to 0.0625
- prefix_keys: bfloat16 [65536, 512], P(('groups', 'seq')), parts along dimension 0, may hold values from -6 to 6
- prefix_values: bfloat16 [65536, 512], P(('groups', 'seq')), parts along dimension 0, may hold values from -6 to 6
- key_scales: float32 [512, 4], P(('groups', 'seq')), parts along dimension 0, may hold values from 1 to 2.5
- value_scales: float32 [512, 4], P(('groups', 'seq')), parts along dimension 0, may hold values from 0.5 to 2
- demo_keys: bfloat16 [32, 2048, 512], P('groups', 'seq'), parts along dimension 0, may hold values from -200 to 200
- demo_values: bfloat16 [32, 2048, 512], P('groups', 'seq'), parts along dimension 0, may hold values from -12 to 12
- task_ids: int32 [64], P('groups'), parts along dimension 0, may hold values from 0 to 15
- demo_lengths: int32 [32], P('groups'), parts along dimension 0, may hold values from 1 to 2048, 16384 in all
- offsets: int32 [64], P('groups'), parts along dimension 0, may hold values from 0 to 31
Outputs:
- mixed: bfloat16 [64, 16384], P('groups', 'seq'), parts along dimension 0
There are 2 independent parts, one for each index of `groups`. A program takes and returns all parts, laid end to end along the dimension named above; an argument that names none is the same for every part. Nothing has to cross between parts.
Inputs may be any that keep to these rules, and one draw needn't show every extreme that they name: `demo_lengths`: the largest is exactly 2048.
All inputs are finite; a program needn't handle non-finite values.
Results may differ from a plain program's by a relative error of at most 0.007.
The roundings to bfloat16 on the way count: a program that leaves them out, or rounds other values in their place, can miss the bound.
Values may be sent and summed in bfloat16 or wider, within the bound.
A program may use at most 128 MiB of HBM per device.

v0:
```python
import functools
import math

import jax
import jax.numpy as jnp
from jax import lax
from jax.experimental import pallas as pl
from jax.experimental.pallas import tpu as pltpu
from jax.sharding import PartitionSpec as P

HD = 128
NEG = -1e30
STAT = 8
F32 = jnp.float32
BF16 = jnp.bfloat16


def remote(src, dst, send, recv, dev):
    return pltpu.make_async_remote_copy(
        src_ref=src,
        dst_ref=dst,
        send_sem=send,
        recv_sem=recv,
        device_id={"seq": dev},
        device_id_type=pl.DeviceIdType.MESH,
    )


def spot(chips, k):
    index = lax.axis_index("seq")
    chip, core = index // 2, lax.rem(index, 2)
    far, near = chip // 2, lax.rem(chip, 2)
    side = lax.rem(1 - near + lax.rem(k, 2), 2)
    return lax.rem(far + 1 + k // 2, chips // 2) * 2 + side


def enter(chips, chip, core):
    barrier = pltpu.get_barrier_semaphore()
    far, near = chip // 2, lax.rem(chip, 2)

    def hello(dev):
        pl.semaphore_signal(
            barrier, inc=1, device_id={"seq": dev}, device_id_type=pl.DeviceIdType.MESH
        )

    def greet(k, _):
        hello((lax.rem(far + k, chips // 2) * 2 + near) * 2 + core)
        return 0

    lax.fori_loop(1, chips // 2, greet, 0)
    hello((far * 2 + 1 - near) * 2 + core)
    hello(chip * 2 + 1 - core)
    pl.semaphore_wait(barrier, chips // 2 + 1)


def gather(chips, chip, core, gat, sem, use):
    z_send, z_recv, y_send, y_recv, f_send, f_recv = sem
    depth = chips // 2
    far, near = chip // 2, lax.rem(chip, 2)

    def from_far(i, side):
        return lax.rem(far - i + depth, depth) * 2 + side

    def move(c, piece, send, recv, dev):
        return remote(gat.at[c, piece], gat.at[c, piece], send, recv, dev)

    def to_far(i):
        dev = (lax.rem(far + i, depth) * 2 + near) * 2 + core
        return move(core, chip, z_send.at[i], z_recv.at[i], dev)

    def of_far(i):
        dev = (lax.rem(far + i, depth) * 2 + near) * 2 + core
        return move(core, from_far(i, near), z_send.at[i], z_recv.at[i], dev)

    def near_copy(i, side):
        dev = (far * 2 + 1 - near) * 2 + core
        return move(core, from_far(i, side), y_send.at[i], y_recv.at[i], dev)

    def core_copy(c, i, e):
        side = near if e == 0 else 1 - near
        k = 2 * i + e
        return move(c, from_far(i, side), f_send.at[k], f_recv.at[k], chip * 2 + 1 - core)

    def start(i, _):
        to_far(i).start()
        return 0

    lax.fori_loop(1, depth, start, 0)
    near_copy(0, near).start()
    core_copy(core, 0, 0).start()

    def forward(i, _):
        of_far(i).wait_recv()
        near_copy(i, near).start()
        core_copy(core, i, 0).start()
        near_copy(i - 1, 1 - near).wait_recv()
        core_copy(core, i - 1, 1).start()
        return 0

    lax.fori_loop(1, depth, forward, 0)
    near_copy(depth - 1, 1 - near).wait_recv()
    core_copy(core, depth - 1, 1).start()

    def arrive(i, _):
        for e in range(2):
            core_copy(1 - core, i, e).wait_recv()
            use(from_far(i, near if e == 0 else 1 - near))
        return 0

    lax.fori_loop(0, depth, arrive, 0)

    def drain(i, _):
        near_copy(i, near).wait_send()
        core_copy(core, i, 0).wait_send()
        core_copy(core, i, 1).wait_send()

        @pl.when(i > 0)
        def _():
            to_far(i).wait_send()

        return 0

    lax.fori_loop(0, depth, drain, 0)


def project_kernel(
    chips, qh, kvs, hid_hbm, wq, wk_hbm, wv_hbm, out,
    hid, wk, wv, wbuf, kvp, part, recv1, sums, recv_y, far_sum, recv_z, gat,
    in_sem, w_sem, s1, r1, sy, ry, sz, rz, *g_sem,
):
    index = lax.axis_index("seq")
    chip, core = index // 2, lax.rem(index, 2)
    depth = chips // 2
    far, near = chip // 2, lax.rem(chip, 2)
    wide = qh * HD
    qt = hid.shape[0] // 2
    kvg = 2 * wk.shape[1] // HD

    def load(k):
        return pltpu.make_async_copy(
            wq.at[:, pl.ds(pl.multiple_of(spot(chips, k) * wide, HD), wide)],
            wbuf.at[k],
            w_sem.at[k],
        )

    def pair(k):
        dev = chip * 2 + 1 - core
        return remote(part.at[1 - core, k], recv1.at[k], s1.at[k], r1.at[k], dev)

    def near_send(i):
        dev = (far * 2 + 1 - near) * 2 + core
        return remote(sums.at[2 * i], recv_y.at[i], sy.at[i], ry.at[i], dev)

    def far_send(i):
        dev = (lax.rem(far + 1 + i, depth) * 2 + near) * 2 + core
        return remote(far_sum.at[i], recv_z.at[i], sz.at[i], rz.at[i], dev)

    small = [
        pltpu.make_async_copy(src, dst, in_sem.at[i])
        for i, (src, dst) in enumerate(((hid_hbm, hid), (wk_hbm, wk), (wv_hbm, wv)))
    ]
    for copy in small:
        copy.start()

    def begin(k, _):
        load(k).start()
        return 0

    lax.fori_loop(0, chips, begin, 0)
    enter(chips, chip, core)
    for copy in small:
        copy.wait()
    for i, w in enumerate((wk, wv)):
        res = jnp.dot(hid[...], w[...], preferred_element_type=F32)
        for g in range(kvg // 2):
            for c in range(2):
                kvp[i * (kvg // 2) + g, c] = res[c * qt : (c + 1) * qt, g * HD : (g + 1) * HD]

    def step(i, _):
        @pl.when(i < depth)
        def _():
            for e in range(2):
                k = 2 * i + e
                load(k).wait()
                res = jnp.dot(hid[...], wbuf[k], preferred_element_type=F32)
                for c in range(2):
                    for s in range(qh):
                        part[c, k, s] = res[c * qt : (c + 1) * qt, s * HD : (s + 1) * HD]
                    for s in range(kvs):
                        part[c, k, qh + s] = kvp[lax.rem(spot(chips, k) * kvs + s, kvg), c]
                pair(k).start()

        @pl.when((i > 0) & (i <= depth))
        def _():
            for e in range(2):
                k = 2 * (i - 1) + e
                pair(k).wait_recv()
                sums[k] = part[core, k] + recv1[k]
                if e == 0:
                    near_send(i - 1).start()

        @pl.when(i > 1)
        def _():
            j = i - 2
            near_send(j).wait_recv()
            far_sum[j] = sums[2 * j + 1] + recv_y[j]

            @pl.when(j < depth - 1)
            def _():
                far_send(j).start()

        return 0

    lax.fori_loop(0, depth + 2, step, 0)

    def collect(i, total):
        far_send(i).wait_recv()
        return total + recv_z[i]

    total = lax.fori_loop(0, depth - 1, collect, far_sum[depth - 1])
    gat[core, chip] = total.astype(BF16)
    gather(chips, chip, core, gat, g_sem, lambda piece: None)

    def drain(i, _):
        pair(2 * i).wait_send()
        pair(2 * i + 1).wait_send()
        near_send(i).wait_send()

        @pl.when(i < depth - 1)
        def _():
            far_send(i).wait_send()

        return 0

    lax.fori_loop(0, depth, drain, 0)
    out[...] = gat[...]


def nt(a, b):
    return lax.dot_general(a, b, (((1,), (1,)), ((), ())), preferred_element_type=F32)


def tn(a, b):
    return lax.dot_general(a, b, (((0,), (0,)), ((), ())), preferred_element_type=F32)


def attend_kernel(
    devices, qh, blk, ks, vs, tasks_of, lens, offs, q_ref, sk, sv, pk, pv, dk, dv, out,
    s_scr, acc, task_row, len_row, s_mask,
):
    h = pl.program_id(0)
    inv = 1.0 / math.sqrt(HD)
    per_head = q_ref.shape[1]
    qt = q_ref.shape[3]
    cols = qh * qt
    rows = 2 * per_head * cols
    q = jnp.concatenate(
        [q_ref[c, p, :qh].reshape(cols, HD) for c in range(2) for p in range(per_head)], axis=0
    )
    blocks = pk.shape[0] // blk
    many = math.gcd(4, blocks)
    tasks, demo_dev = dk.shape[0], dk.shape[1]
    some = math.gcd(4, tasks)

    @pl.when(h == 0)
    def _():
        index = lax.axis_index("seq")
        lane = lax.broadcasted_iota(jnp.int32, (1, rows), 1)
        token = (lane // (rows // 2)) * qt + lax.rem(lane, qt)
        zero = jnp.zeros((1, rows), jnp.int32)

        def spread(t, carry):
            task = tasks_of[t]
            here = token == t
            left = lens[task] - index * demo_dev
            values = (task, left, offs[t])
            return tuple(jnp.where(here, v, old) for v, old in zip(values, carry))

        task_all, len_all, off_all = lax.fori_loop(0, 2 * qt, spread, (zero, zero, zero))
        task_row[...] = task_all
        len_row[...] = len_all

        def allow(u, _):
            mine = jnp.where(lax.rem(u, devices) == index, tasks_of[u], -1)
            keep = (task_all == mine) & (off_all >= offs[u])
            s_mask[pl.ds(u, 1), :] = keep.astype(jnp.int32)
            return 0

        lax.fori_loop(0, 2 * qt, allow, 0)

    def fold(x, op):
        return op(x.reshape(x.shape[0] // 8, 8, x.shape[1]), axis=0)

    def score(i, top):
        for b in range(many):
            at = i * many + b
            here = pl.ds(pl.multiple_of(at * blk, blk), blk)
            s = nt(pk[here, :], q) * (ks[h, at] * inv)
            s_scr[here, :] = s
            top = jnp.maximum(top, fold(s, jnp.max))
        return top

    top = lax.fori_loop(0, blocks // many, score, jnp.full((8, rows), NEG, F32))
    mine = task_row[...]

    def pick(i, best):
        for b in range(some):
            best = jnp.where(mine == i * some + b, nt(dk[i * some + b], q), best)
        return best

    s_demo = lax.fori_loop(0, tasks // some, pick, jnp.zeros((demo_dev, rows), F32))
    slot = lax.broadcasted_iota(jnp.int32, (demo_dev, rows), 0)
    s_demo = jnp.where(slot < len_row[...], s_demo * inv, NEG)
    self_k = jnp.concatenate([sk[c, 0, 0] for c in range(2)], axis=0)
    self_v = jnp.concatenate([sv[c, 0, 0] for c in range(2)], axis=0)
    s_self = jnp.where(s_mask[...] > 0, nt(self_k, q) * inv, NEG)
    top = jnp.maximum(top, jnp.maximum(fold(s_demo, jnp.max), fold(s_self, jnp.max)))
    top = jnp.max(top, axis=0, keepdims=True)

    e_demo = jnp.exp(s_demo - top)
    e_self = jnp.exp(s_self - top)
    total = fold(e_demo, jnp.sum) + fold(e_self, jnp.sum)
    acc[...] = tn(self_v, e_self.astype(BF16))

    def demo(i, _):
        weights = jnp.concatenate(
            [jnp.where(mine == i * some + b, e_demo, 0.0).astype(BF16) for b in range(some)], axis=0
        )
        here = pl.ds(i * some, some)
        acc[...] += tn(dv[here].reshape(some * demo_dev, HD), weights)
        return 0

    lax.fori_loop(0, tasks // some, demo, 0)

    def prefix(i, total):
        weights = []
        for b in range(many):
            at = i * many + b
            e = jnp.exp(s_scr[pl.ds(pl.multiple_of(at * blk, blk), blk), :] - top)
            total = total + fold(e, jnp.sum)
            weights.append((e * vs[h, at]).astype(BF16))
        here = pl.ds(pl.multiple_of(i * many * blk, blk), many * blk)
        acc[...] += tn(pv[here, :], jnp.concatenate(weights, axis=0))
        return total

    total = lax.fori_loop(0, blocks // many, prefix, total)
    total = jnp.sum(total, axis=0, keepdims=True)
    first = lax.broadcasted_iota(jnp.int32, (STAT, rows), 0) == 0
    stats = jnp.where(first, top, total)
    for c in range(2):
        for p in range(per_head):
            lanes = slice((c * per_head + p) * cols, (c * per_head + p + 1) * cols)
            out[c, p, :HD] = acc[:, lanes]
            out[c, p, HD:] = stats[:, lanes]


def output_kernel(
    chips, qh, part, wo, out,
    wbuf, recv1, keep, y_val, y_stat, yr_val, yr_stat, z_val, z_stat, zr_val, zr_stat, gat, acc,
    w_sem, s1, r1, sy, ry, sz, rz, sy2, ry2, sz2, rz2, *g_sem,
):
    index = lax.axis_index("seq")
    chip, core = index // 2, lax.rem(index, 2)
    depth = chips // 2
    far, near = chip // 2, lax.rem(chip, 2)
    deep = qh * HD
    cols = part.shape[3]
    qt = cols // qh

    def load(k):
        return pltpu.make_async_copy(
            wo.at[pl.ds(pl.multiple_of(k * deep, HD), deep), :], wbuf.at[k], w_sem.at[k]
        )

    def pair(k):
        dev = chip * 2 + 1 - core
        src = part.at[1 - core, spot(chips, k)]
        return remote(src, recv1.at[k], s1.at[k], r1.at[k], dev)

    def near_send(i):
        dev = (far * 2 + 1 - near) * 2 + core
        return (
            remote(y_stat.at[i], yr_stat.at[i], sy2.at[i], ry2.at[i], dev),
            remote(y_val.at[i], yr_val.at[i], sy.at[i], ry.at[i], dev),
        )

    def far_send(i):
        dev = (lax.rem(far + 1 + i, depth) * 2 + near) * 2 + core
        return (
            remote(z_stat.at[i], zr_stat.at[i], sz2.at[i], rz2.at[i], dev),
            remote(z_val.at[i], zr_val.at[i], sz.at[i], rz.at[i], dev),
        )

    enter(chips, chip, core)

    def begin(k, _):
        pair(k).start()
        return 0

    lax.fori_loop(0, chips, begin, 0)

    def begin_load(k, _):
        load(k).start()
        return 0

    lax.fori_loop(0, chips, begin_load, 0)
    first = lax.broadcasted_iota(jnp.int32, (STAT, cols), 0) == 0

    def join(a, a_stat, b, b_stat):
        top = jnp.maximum(a_stat[:1], b_stat[:1])
        fa, fb = jnp.exp(a_stat[:1] - top), jnp.exp(b_stat[:1] - top)
        stat = jnp.where(first, top, a_stat * fa + b_stat * fb)
        return a.astype(F32) * fa + b.astype(F32) * fb, stat

    def merge(k):
        pair(k).wait_recv()
        at = spot(chips, k)
        return join(part[core, at, :HD], part[core, at, HD:], recv1[k, :HD], recv1[k, HD:])

    def step(i, _):
        @pl.when(i < depth)
        def _():
            value, stat = merge(2 * i)
            y_val[i] = value.astype(BF16)
            y_stat[i] = stat
            for copy in near_send(i):
                copy.start()
            value, stat = merge(2 * i + 1)
            keep[i, :HD] = value
            keep[i, HD:] = stat

        @pl.when(i > 0)
        def _():
            j = i - 1
            for copy in near_send(j):
                copy.wait_recv()
            value, stat = join(keep[j, :HD], keep[j, HD:], yr_val[j], yr_stat[j])

            @pl.when(j < depth - 1)
            def _():
                z_val[j] = value.astype(BF16)
                z_stat[j] = stat
                for copy in far_send(j):
                    copy.start()

            @pl.when(j == depth - 1)
            def _():
                keep[j, :HD] = value
                keep[j, HD:] = stat

        return 0

    lax.fori_loop(0, depth + 1, step, 0)

    def arrive(i, _):
        for copy in far_send(i):
            copy.wait_recv()
        return 0

    lax.fori_loop(0, depth - 1, arrive, 0)
    own = depth - 1
    top = keep[own, HD : HD + 1]
    for k in range(own):
        top = jnp.maximum(top, zr_stat[k, :1])
    factor = jnp.exp(keep[own, HD : HD + 1] - top)
    total = keep[own, HD + 1 : HD + 2] * factor
    value = keep[own, :HD] * factor
    for k in range(own):
        factor = jnp.exp(zr_stat[k, :1] - top)
        total = total + zr_stat[k, 1:2] * factor
        value = value + zr_val[k].astype(F32) * factor
    rows = (value / total).T.astype(BF16)
    gat[core, chip] = rows.reshape(qh, qt, HD)
    acc[...] = jnp.zeros_like(acc)

    def mix(piece):
        load(piece).wait()
        left = jnp.concatenate(
            [
                jnp.concatenate([gat[c, piece, s] for s in range(qh)], axis=1)
                for c in range(2)
            ],
            axis=0,
        )
        acc[...] += jnp.dot(left, wbuf[piece], preferred_element_type=F32)

    gather(chips, chip, core, gat, g_sem, mix)

    def drain(i, _):
        pair(2 * i).wait_send()
        pair(2 * i + 1).wait_send()
        for copy in near_send(i):
            copy.wait_send()

        @pl.when(i < depth - 1)
        def _():
            for copy in far_send(i):
                copy.wait_send()

        return 0

    lax.fori_loop(0, depth, drain, 0)
    out[...] = acc[...].astype(BF16)


def sems(*counts):
    return [pltpu.SemaphoreType.DMA((n,)) for n in counts]


def body(
    hidden, w_query, w_key, w_value, w_out, prefix_keys, prefix_values, key_scales, value_scales,
    demo_keys, demo_values, task_ids, demo_lengths, offsets,
):
    devices = lax.axis_size("seq")
    chips = devices // 2
    half = chips // 2
    qtok, depth = hidden.shape
    qt = qtok // 2
    kvh = prefix_keys.shape[1] // HD
    heads = w_query.shape[1] // HD
    group = heads // kvh
    qh = heads // chips
    kvs = max(1, 2 * kvh // chips)
    gp = qh + kvs
    cols = qh * qt
    per_head = chips // kvh
    tasks, demo_dev = demo_keys.shape[:2]
    pre_dev = prefix_keys.shape[0]
    blk = pre_dev // key_scales.shape[0]
    rows = qtok * group
    vmem = pl.BlockSpec(memory_space=pltpu.VMEM)
    hbm = pl.BlockSpec(memory_space=pltpu.HBM)

    query = pl.pallas_call(
        functools.partial(project_kernel, chips, qh, kvs),
        name="project",
        out_shape=jax.ShapeDtypeStruct((2, chips, gp, qt, HD), BF16),
        in_specs=[hbm, hbm, hbm, hbm],
        out_specs=vmem,
        scratch_shapes=[
            pltpu.VMEM(hidden.shape, BF16),
            pltpu.VMEM(w_key.shape, BF16),
            pltpu.VMEM(w_value.shape, BF16),
            pltpu.VMEM((chips, depth, qh * HD), BF16),
            pltpu.VMEM((2 * kvh, 2, qt, HD), F32),
            pltpu.VMEM((2, chips, gp, qt, HD), F32),
            pltpu.VMEM((chips, gp, qt, HD), F32),
            pltpu.VMEM((chips, gp, qt, HD), F32),
            pltpu.VMEM((half, gp, qt, HD), F32),
            pltpu.VMEM((half, gp, qt, HD), F32),
            pltpu.VMEM((half, gp, qt, HD), F32),
            pltpu.VMEM((2, chips, gp, qt, HD), BF16),
        ]
        + sems(3, chips, chips, chips, *[half] * 8, chips, chips),
        compiler_params=pltpu.CompilerParams(
            collective_id=0, has_side_effects=True, vmem_limit_bytes=48 << 20
        ),
    )(hidden, w_query, w_key, w_value)

    def kv_spec(first):
        return pl.BlockSpec(
            (2, 1, 1, qt, HD),
            lambda h: (0, (first + h) // kvs, qh + (first + h) % kvs, 0, 0),
        )

    smem = pl.BlockSpec(memory_space=pltpu.SMEM)
    pre_spec = pl.BlockSpec((pre_dev, HD), lambda h: (0, h))
    demo_spec = pl.BlockSpec((tasks, demo_dev, HD), lambda h: (0, 0, h))
    part = pl.pallas_call(
        functools.partial(attend_kernel, devices, qh, blk),
        name="attend",
        grid=(kvh,),
        out_shape=jax.ShapeDtypeStruct((2, chips, HD + STAT, cols), F32),
        in_specs=[
            *[smem] * 5,
            pl.BlockSpec((2, per_head, gp, qt, HD), lambda h: (0, h, 0, 0, 0)),
            kv_spec(0),
            kv_spec(kvh),
            pre_spec,
            pre_spec,
            demo_spec,
            demo_spec,
        ],
        out_specs=pl.BlockSpec((2, per_head, HD + STAT, cols), lambda h: (0, h, 0, 0)),
        scratch_shapes=[
            pltpu.VMEM((pre_dev, rows), F32),
            pltpu.VMEM((HD, rows), F32),
            pltpu.VMEM((1, rows), jnp.int32),
            pltpu.VMEM((1, rows), jnp.int32),
            pltpu.VMEM((qtok, rows), jnp.int32),
        ],
        compiler_params=pltpu.CompilerParams(vmem_limit_bytes=40 << 20),
    )(
        key_scales.T, value_scales.T, task_ids, demo_lengths, offsets, query, query, query,
        prefix_keys, prefix_values, demo_keys, demo_values,
    )

    return pl.pallas_call(
        functools.partial(output_kernel, chips, qh),
        name="mix",
        out_shape=jax.ShapeDtypeStruct((qtok, w_out.shape[1]), BF16),
        in_specs=[vmem, hbm],
        out_specs=vmem,
        scratch_shapes=[
            pltpu.VMEM((chips, qh * HD, w_out.shape[1]), BF16),
            pltpu.VMEM((chips, HD + STAT, cols), F32),
            pltpu.VMEM((half, HD + STAT, cols), F32),
            *[
                pltpu.VMEM((half, extent, cols), kind)
                for _ in range(4)
                for extent, kind in ((HD, BF16), (STAT, F32))
            ],
            pltpu.VMEM((2, chips, qh, qt, HD), BF16),
            pltpu.VMEM((qtok, w_out.shape[1]), F32),
        ]
        + sems(chips, chips, chips, *[half] * 12, chips, chips),
        compiler_params=pltpu.CompilerParams(
            collective_id=1, has_side_effects=True, vmem_limit_bytes=48 << 20
        ),
    )(part, w_out)


def solution(mesh):
    placed = (
        P("groups", "seq"),
        P("seq", None),
        P("seq", None),
        P("seq", None),
        P(None, "seq"),
        P(("groups", "seq"), None),
        P(("groups", "seq"), None),
        P(("groups", "seq"), None),
        P(("groups", "seq"), None),
        P("groups", "seq", None),
        P("groups", "seq", None),
        P("groups"),
        P("groups"),
        P("groups"),
    )
    return jax.shard_map(
        body, mesh=mesh, in_specs=placed, out_specs=P("groups", "seq"), check_vma=False
    )
```

profile of v0, /device:TPU:0, one launch (start us, length us, event | category | flops | bytes accessed | tf_op | source)
XLA Modules:
  0.0 88.2 jit_solution(1681441171785263536)
XLA Ops:
  0.0 0.0 copy-start.4
  0.0 1.2 %copy-done.4 = bf16[1024,512]{1,0:T(8,128)(2,1)S(1)} copy-done((bf16[1024,512]{1,0:T(8,128)(2,1)S(1)}, bf16[1024,512]{1,0:T(8,128)(2,1)}, u32[]{:S(2)}) %copy-start.4) | copy-done | bytes 1048600
  1.2 0.0 copy-start.5
  1.2 1.2 %copy-done.5 = bf16[1024,512]{1,0:T(8,128)(2,1)S(1)} copy-done((bf16[1024,512]{1,0:T(8,128)(2,1)S(1)}, bf16[1024,512]{1,0:T(8,128)(2,1)}, u32[]{:S(2)}) %copy-start.5) | copy-done | bytes 1048600
  2.5 0.0 copy-start.6
  2.5 0.8 copy-done.6
  3.3 0.0 copy-start
  3.3 0.0 copy-start.1
  3.3 0.0 copy-start.2
  3.3 0.0 copy-start.3
  3.3 0.0 copy-start.7
  3.3 0.0 copy-start.8
  3.3 0.0 copy-start.9
  3.3 0.0 copy-start.10
  3.3 0.0 copy-start.11
  3.4 32.8 %project.1.q_ref.sk.sv = bf16[2,8,9,16,128]{4,3,2,1,0:T(8,128)(2,1)S(1)} custom-call(bf16[32,1024]{1,0:T(8,128)(2,1)S(1)} %copy-done.6, bf16[1024,8192]{1,0:T(8,128)(2,1)} %wq.1, bf16[1024,512]{1,0:T(8,128)(2,1)S(1)} %copy-done.4, bf16[1024,512]{1,0:T(8,128)(2,1)S(1)} %copy-done.5), custom_call_target="tpu_custom_call" | custom-call | tf_op jit(solution)/shard_map/project/pallas_call | solution.py:534
  36.2 0.0 copy-done
  36.2 0.0 copy-done.1
  36.2 0.0 copy-done.2
  36.2 0.0 copy-done.3
  36.2 0.0 copy-done.7
  36.2 0.0 copy-done.8
  36.2 0.0 copy-done.9
  36.2 0.0 copy-done.10
  36.2 0.0 copy-done.11
  36.3 24.4 %attend.1.part = f32[2,8,136,128]{3,2,1,0:T(8,128)S(1)} custom-call(f32[4,16]{1,0:T(4,128)S(1)} %bitcast.2, f32[4,16]{1,0:T(4,128)S(1)} %bitcast.3, s32[32]{0:T(128)S(1)} %copy-done.9, s32[16]{0:T(128)S(1)} %copy-done.10, s32[32]{0:T(128)S(1)} %copy-done.11, bf16[2,8,9,16,128]{4,3,2,1,0:T(8,128)(2,1)S(1)} %project.1.q_ref.sk.sv, ...), custom_call_target="tpu_custom_call" | custom-call | tf_op jit(solution)/shard_map/attend/pallas_call | solution.py:569
  60.6 26.9 %mix.1 = bf16[32,1024]{1,0:T(8,128)(2,1)S(1)} custom-call(f32[2,8,136,128]{3,2,1,0:T(8,128)S(1)} %attend.1.part, bf16[8192,1024]{1,0:T(8,128)(2,1)} %wo.1), custom_call_target="tpu_custom_call" | custom-call | tf_op jit(solution)/shard_map/mix/pallas_call | solution.py:598
  87.5 0.6 copy.16
Async XLA Ops:
  0.0 1.2 %copy-start.4 = (bf16[1024,512]{1,0:T(8,128)(2,1)S(1)}, bf16[1024,512]{1,0:T(8,128)(2,1)}, u32[]{:S(2)}) copy-start(bf16[1024,512]{1,0:T(8,128)(2,1)} %wk_hbm.1) | copy-start | bytes 3145732
  1.2 1.2 %copy-start.5 = (bf16[1024,512]{1,0:T(8,128)(2,1)S(1)}, bf16[1024,512]{1,0:T(8,128)(2,1)}, u32[]{:S(2)}) copy-start(bf16[1024,512]{1,0:T(8,128)(2,1)} %wv_hbm.1) | copy-start | bytes 3145732
  2.5 0.8 copy-start.6
  3.3 32.9 %copy-start = (bf16[2048,512]{1,0:T(8,128)(2,1)S(1)}, bf16[2048,512]{1,0:T(8,128)(2,1)}, u32[]{:S(2)}) copy-start(bf16[2048,512]{1,0:T(8,128)(2,1)} %pk.1) | copy-start | bytes 6291460
  3.3 32.9 %copy-start.1 = (bf16[2048,512]{1,0:T(8,128)(2,1)S(1)}, bf16[2048,512]{1,0:T(8,128)(2,1)}, u32[]{:S(2)}) copy-start(bf16[2048,512]{1,0:T(8,128)(2,1)} %pv.1) | copy-start | bytes 6291460
  3.3 32.9 %copy-start.2 = (bf16[16,128,512]{2,1,0:T(8,128)(2,1)S(1)}, bf16[16,128,512]{2,1,0:T(8,128)(2,1)}, u32[]{:S(2)}) copy-start(bf16[16,128,512]{2,1,0:T(8,128)(2,1)} %dk.1) | copy-start | bytes 6291460
  3.3 32.9 %copy-start.3 = (bf16[16,128,512]{2,1,0:T(8,128)(2,1)S(1)}, bf16[16,128,512]{2,1,0:T(8,128)(2,1)}, u32[]{:S(2)}) copy-start(bf16[16,128,512]{2,1,0:T(8,128)(2,1)} %dv.1) | copy-start | bytes 6291460
  3.3 32.9 %copy-start.7 = (f32[16,4]{0,1:T(4,128)S(1)}, f32[16,4]{0,1:T(4,128)}, u32[]{:S(2)}) copy-start(f32[16,4]{0,1:T(4,128)} %param.21) | copy-start | bytes 772
  3.3 32.9 %copy-start.8 = (f32[16,4]{0,1:T(4,128)S(1)}, f32[16,4]{0,1:T(4,128)}, u32[]{:S(2)}) copy-start(f32[16,4]{0,1:T(4,128)} %param.22) | copy-start | bytes 772
  3.3 32.9 %copy-start.9 = (s32[32]{0:T(128)S(1)}, s32[32]{0:T(128)}, u32[]{:S(2)}) copy-start(s32[32]{0:T(128)} %tasks_of.1) | copy-start | bytes 388
  3.3 32.9 %copy-start.10 = (s32[16]{0:T(128)S(1)}, s32[16]{0:T(128)}, u32[]{:S(2)}) copy-start(s32[16]{0:T(128)} %lens.1) | copy-start | bytes 196
  3.3 32.9 %copy-start.11 = (s32[32]{0:T(128)S(1)}, s32[32]{0:T(128)}, u32[]{:S(2)}) copy-start(s32[32]{0:T(128)} %offs.1) | copy-start | bytes 388
where the time goes:
time: 88.4 us; the launch traced here: 88.2 us
  Pallas kernels  84.1 us (95%)
  local copies, waits for them, and re-layouts  3.96 us (4%)
    pallas_call x1, Pallas kernels, body(): pl.pallas_call(functools.partial(project_kernel, chips, qh, kvs), name='p...  32.8 us
    pallas_call x1, Pallas kernels, body(): pl.pallas_call(functools.partial(output_kernel, chips, qh), name='mix', o...  26.9 us
    pallas_call x1, Pallas kernels, body(): pl.pallas_call(functools.partial(attend_kernel, devices, qh, blk), name='...  24.4 us
    unnamed x25, local copies, waits for them, and re-layouts  3.96 us

commit v1 on v0

v1 whole, which is shorter than its diff:
```python
import functools
import math
import types

import jax
import jax.numpy as jnp
from jax import lax
from jax.experimental import pallas as pl
from jax.experimental.pallas import tpu as pltpu
from jax.sharding import PartitionSpec as P

HD = 128
NEG = -1e30
SIDES = 2
STAT = 8
F32 = jnp.float32
BF16 = jnp.bfloat16


def nt(a, b):
    return lax.dot_general(a, b, (((1,), (1,)), ((), ())), preferred_element_type=F32)


def nn(a, b):
    return jnp.dot(a, b, preferred_element_type=F32)


def loop(n, step):
    def wrapped(i, carry):
        step(i)
        return carry

    lax.fori_loop(0, n, wrapped, 0)


def remote(src, dst, send, recv, dev):
    return pltpu.make_async_remote_copy(
        src_ref=src,
        dst_ref=dst,
        send_sem=send,
        recv_sem=recv,
        device_id={"seq": dev},
        device_id_type=pl.DeviceIdType.MESH,
    )


def kernel(cfg, names, *refs):
    r = types.SimpleNamespace(**dict(zip(names, refs)))
    kvh, group, half, devices = cfg.kvh, cfg.group, cfg.half, cfg.devices
    tq, tz, qtok, blk, rows = cfg.tq, cfg.tz, cfg.qtok, cfg.blk, cfg.rows
    nch, cw = cfg.nch, cfg.cw
    index = lax.axis_index("seq")
    chip, core = index // 2, lax.rem(index, 2)
    far, near = chip // SIDES, lax.rem(chip, SIDES)
    const = math.log2(math.e) / math.sqrt(HD)

    def device(f, n, c):
        return (f * SIDES + n) * 2 + c

    partner = device(far, near, 1 - core)
    across = device(far, 1 - near, core)

    def up(i):
        return lax.rem(far + i, half)

    def down(i):
        return lax.rem(far - i + half, half)

    def load_wq(k):
        src = r.wq.at[:, pl.ds(pl.multiple_of(k * cw, HD), cw)]
        return pltpu.make_async_copy(src, r.wqb.at[k], r.s_wq.at[k])

    def load_wo(h):
        deep = group * HD
        src = r.wo.at[pl.ds(pl.multiple_of(h * deep, HD), deep), :]
        return pltpu.make_async_copy(src, r.wob.at[h], r.s_wo.at[h])

    def load_cache(h):
        lanes = pl.ds(pl.multiple_of(h * HD, HD), HD)
        return (
            pltpu.make_async_copy(r.pk.at[:, lanes], r.pkb.at[h], r.s_pk.at[h]),
            pltpu.make_async_copy(r.dk.at[:, :, lanes], r.dkb.at[h], r.s_dk.at[h]),
            pltpu.make_async_copy(r.pv.at[:, lanes], r.pvb.at[h], r.s_pv.at[h]),
            pltpu.make_async_copy(r.dv.at[:, :, lanes], r.dvb.at[h], r.s_dv.at[h]),
        )

    small = [
        pltpu.make_async_copy(src, dst, r.s_in.at[i])
        for i, (src, dst) in enumerate(((r.hid, r.hidb), (r.wk, r.wkb), (r.wv, r.wvb)))
    ]
    small[0].start()
    loop(nch, lambda k: load_wq(k).start())
    small[1].start()
    small[2].start()
    loop((kvh - 1) * nch, lambda k: load_wq(k + nch).start())

    barrier = pltpu.get_barrier_semaphore()

    def greet(k):
        pl.semaphore_signal(
            barrier,
            inc=1,
            device_id={"seq": lax.rem(index + 1 + k, devices)},
            device_id_type=pl.DeviceIdType.MESH,
        )

    loop(devices - 1, greet)

    lane_d = lax.broadcasted_iota(jnp.int32, (1, cfg.demo_dev), 1)
    lane_t = lax.broadcasted_iota(jnp.int32, (1, qtok), 1)

    def spread(t, carry):
        here = lane_t == t
        return tuple(jnp.where(here, v[t], old) for v, old in zip((r.tasks, r.offs), carry))

    zero = jnp.zeros((1, qtok), jnp.int32)
    task_all, off_all = lax.fori_loop(0, qtok, spread, (zero, zero))
    mine = lax.rem(lane_t, devices) == index

    def mask(t):
        task = r.tasks[t]
        left = r.lens[task] - index * cfg.demo_dev
        r.dmask[pl.ds(t, 1), :] = jnp.where(lane_d < left, 0.0, NEG)
        keep = mine & (task_all == task) & (off_all <= r.offs[t])
        r.smask[pl.ds(t, 1), :] = jnp.where(keep, 0.0, NEG)

    loop(qtok, mask)
    r.gs[...] = jnp.zeros_like(r.gs)
    r.acc[...] = jnp.zeros_like(r.acc)
    small[0].wait()

    def project(h):
        def chunk(n):
            k = h * nch + n
            load_wq(k).wait()
            res = nn(r.hidb[...], r.wqb[k])
            per = cw // HD
            for c in range(2):
                for s in range(SIDES):
                    at = (c * SIDES + s) * tq
                    for u in range(per):
                        r.part[h, c, s, n * per + u] = res[at : at + tq, u * HD : (u + 1) * HD]

        loop(nch, chunk)

    def project_kv():
        for copy in small[1:]:
            copy.wait()
        for e, w in enumerate((r.wkb, r.wvb)):
            res = nn(r.hidb[...], w[...])
            for c in range(2):
                for s in range(SIDES):
                    at = (c * SIDES + s) * tq
                    for h in range(kvh):
                        r.kpart[c, s, 2 * h + e] = res[at : at + tq, h * HD : (h + 1) * HD]

    def pair(h):
        return remote(r.part.at[h, 1 - core], r.recv1.at[h], r.s1.at[h], r.r1.at[h], partner)

    def pair_kv():
        return remote(r.kpart.at[1 - core], r.krecv1, r.ks1.at[0], r.kr1.at[0], partner)

    def cross(h):
        return remote(r.ysum.at[h], r.yrecv.at[h], r.sy.at[h], r.ry.at[h], across)

    def cross_kv():
        return remote(r.kysum, r.kyrecv, r.ksy.at[0], r.kry.at[0], across)

    def long(h, i):
        return remote(
            r.zbuf.at[h, pl.ds(up(i) * tz, tz)], r.zrecv.at[h, i - 1],
            r.sz.at[h, i - 1], r.rz.at[h, i - 1], device(up(i), near, core),
        )

    def long_kv(i):
        return remote(
            r.kz.at[pl.ds(up(i) * cfg.kuz, cfg.kuz)], r.kzrecv.at[i - 1],
            r.ksz.at[i - 1], r.krz.at[i - 1], device(up(i), near, core),
        )

    def side(k):
        return lax.rem(near + lax.rem(k, 2), 2)

    def spreading(buf, send, recv, k):
        dev = device(up(k // 2), side(k), core)
        piece = buf.at[core, near, far]
        return remote(piece, piece, send.at[k], recv.at[k], dev)

    def landing(buf, send, recv, k):
        dev = device(up(k // 2), side(k), core)
        piece = buf.at[core, side(k), down(k // 2)]
        return remote(piece, piece, send.at[k], recv.at[k], dev)

    def forward(buf, send, recv):
        return remote(buf.at[core], buf.at[core], send, recv, partner)

    def arrived(buf, send, recv):
        return remote(buf.at[1 - core], buf.at[1 - core], send, recv, partner)

    chips = SIDES * half

    def spread_out(buf, send, recv):
        loop(chips - 1, lambda k: spreading(buf, send, recv, k + 1).start())

    def pass_on(buf, send, recv, fsend, frecv):
        loop(chips - 1, lambda k: landing(buf, send, recv, k + 1).wait_recv())
        forward(buf, fsend, frecv).start()

    def q_gather(h):
        return r.gat.at[h], r.sg.at[h], r.rg.at[h]

    def kv_gather():
        return r.gkv, r.ksg, r.krg

    def o_gather(h):
        return r.agat.at[h], r.sa.at[h], r.ra.at[h]

    def stage_b(h):
        pair(h).wait_recv()
        r.ysum[h] = r.part[h, core, 1 - near] + r.recv1[h, 1 - near]
        cross(h).start()
        r.own[h] = r.part[h, core, near] + r.recv1[h, near]

    def stage_b_kv():
        pair_kv().wait_recv()
        r.kysum[...] = r.kpart[core, 1 - near] + r.krecv1[1 - near]
        cross_kv().start()
        r.kown[...] = r.kpart[core, near] + r.krecv1[near]

    def stage_c(h):
        cross(h).wait_recv()
        r.zbuf[h] = jnp.swapaxes(r.own[h] + r.yrecv[h], 0, 1)
        loop(half - 1, lambda i: long(h, i + 1).start())

    def stage_c_kv():
        cross_kv().wait_recv()
        r.kz[...] = r.kown[...] + r.kyrecv[...]
        loop(half - 1, lambda i: long_kv(i + 1).start())

    def stage_d(h):
        total = r.zbuf[h, pl.ds(far * tz, tz)]
        for i in range(1, half):
            long(h, i).wait_recv()
            total = total + r.zrecv[h, i - 1]
        r.gat[h, core, near, far] = total.astype(BF16)
        spread_out(*q_gather(h))

    def stage_d_kv():
        total = r.kz[pl.ds(far * cfg.kuz, cfg.kuz)]
        for i in range(1, half):
            long_kv(i).wait_recv()
            total = total + r.kzrecv[i - 1]
        r.gkv[core, near, far] = total.astype(BF16)
        spread_out(*kv_gather())

    def stage_e(h):
        pass_on(*q_gather(h), r.sf.at[h], r.rf.at[h])

    def front(i):
        @pl.when(i < kvh)
        def _():
            project(i)
            pair(i).start()

        @pl.when(i < kvh + 1)
        def _():
            stage_b(i - 1)

        @pl.when(i == 1)
        def _():
            stage_b_kv()

        @pl.when((i >= 3) & (i < kvh + 3))
        def _():
            stage_c(i - 3)

        @pl.when(i == 3)
        def _():
            stage_c_kv()

            def caches(h):
                for copy in load_cache(h):
                    copy.start()

            loop(kvh, caches)
            loop(kvh, lambda h: load_wo(h).start())

        @pl.when(i >= 5)
        def _():
            stage_d(i - 5)

        @pl.when(i == 5)
        def _():
            stage_d_kv()

    project(0)
    pl.semaphore_wait(barrier, devices - 1)
    pair(0).start()
    project_kv()
    pair_kv().start()
    loop(kvh + 4, lambda i: front(i + 1))
    stage_e(0)
    pass_on(*kv_gather(), r.ksf.at[0], r.krf.at[0])
    arrived(r.gkv, r.ksf.at[0], r.krf.at[0]).wait_recv()

    def out_send(h, b, k):
        c, s = b // SIDES, b % SIDES
        dev = device(up(k), s, c)
        return (
            remote(
                r.oval.at[h, b, up(k)], r.rval.at[h, index],
                r.so.at[h, b * half + k], r.ro.at[h, index], dev,
            ),
            remote(
                r.ostat.at[h, b], r.rstat.at[h, index],
                r.st.at[h, b * half + k], r.rt.at[h, index], dev,
            ),
        )

    def is_me(b, k):
        return (k == 0) & (core == b // SIDES) & (near == b % SIDES)

    def out_from(h, dev):
        return (
            remote(r.oval.at[h, 0, 0], r.rval.at[h, dev], r.so.at[h, 0], r.ro.at[h, dev], dev),
            remote(r.ostat.at[h, 0], r.rstat.at[h, dev], r.st.at[h, 0], r.rt.at[h, dev], dev),
        )

    width = 2 * blk
    steps = cfg.pre_dev // width
    blocks = 2 * SIDES

    def attend(h, between):
        def query(b):
            return r.gat[h, b // SIDES, b % SIDES].reshape(rows, HD)

        def self_kv(e):
            unit = 2 * h + e
            f, j = unit // cfg.kuz, lax.rem(unit, cfg.kuz)
            return jnp.concatenate(
                [r.gkv[c, s, f, j] for c in range(2) for s in range(SIDES)], axis=0
            )

        self_k, self_v = self_kv(0), self_kv(1)

        def score(b, j, q, run):
            s = nt(q, r.pkb[h, j * width : (j + 1) * width, :])
            for e in range(2):
                at = 2 * j + e
                x = s[:, e * blk : (e + 1) * blk] * (r.ks[h, at] * const)
                r.scr[b % 2][:, at * blk : (at + 1) * blk] = x
                run = jnp.maximum(run, x)
            return run

        def small_scores(b, q):
            demo, bias = [], []
            for t in range(tq):
                tok = b * tq + t
                k = r.dkb[h, r.tasks[tok]]
                s = nt(q[t * group : (t + 1) * group], k) * const
                demo.append(s + r.dmask[tok : tok + 1, :])
                bias.append(jnp.broadcast_to(r.smask[tok : tok + 1, :], (group, qtok)))
            own = nt(q, self_k) * const + jnp.concatenate(bias, axis=0)
            return jnp.concatenate(demo, axis=0), own

        def first(b):
            return jnp.full((rows, blk), NEG, F32)

        q = query(0)
        run = first(0)
        for j in range(steps):
            run = score(0, j, q, run)
        for b in range(blocks):
            s_demo, s_self = small_scores(b, q)
            top = jnp.maximum(
                jnp.max(run, axis=1, keepdims=True),
                jnp.maximum(
                    jnp.max(s_demo, axis=1, keepdims=True), jnp.max(s_self, axis=1, keepdims=True)
                ),
            )
            e_demo, e_self = jnp.exp2(s_demo - top), jnp.exp2(s_self - top)
            total = jnp.sum(e_demo, axis=1, keepdims=True) + jnp.sum(e_self, axis=1, keepdims=True)
            w_demo, w_self = e_demo.astype(BF16), e_self.astype(BF16)
            sums = jnp.zeros((rows, blk), F32)
            if b + 1 < blocks:
                q = query(b + 1)
                run = first(b + 1)
            for j in range(steps):
                for e in range(2):
                    at = 2 * j + e
                    lanes = slice(at * blk, (at + 1) * blk)
                    x = jnp.exp2(r.scr[b % 2][:, lanes] - top)
                    sums = sums + x
                    r.wts[b % 2][:, lanes] = (x * r.vs[h, at]).astype(BF16)
                if b + 1 < blocks:
                    run = score(b + 1, j, q, run)
            total = total + jnp.sum(sums, axis=1, keepdims=True)
            value = nn(r.wts[b % 2][...], r.pvb[h]) + nn(w_self, self_v)
            value = value + jnp.concatenate(
                [
                    nn(w_demo[t * group : (t + 1) * group], r.dvb[h, r.tasks[b * tq + t]])
                    for t in range(tq)
                ],
                axis=0,
            )
            lane = lax.broadcasted_iota(jnp.int32, (rows, HD), 1)
            r.ostat[h, b] = jnp.where(lane == 0, top, total).T[:STAT]
            r.oval[h, b] = value.astype(BF16).reshape(half, tz * group, HD)

            def ship(k):
                @pl.when(jnp.logical_not(is_me(b, k)))
                def _():
                    for copy in out_send(h, b, k):
                        copy.start()

            loop(half, ship)
            between(b)

    def join(h):
        def take(k):
            for copy in out_from(h, lax.rem(index + 1 + k, devices)):
                copy.wait_recv()

        loop(devices - 1, take)
        mine_b = core * SIDES + near
        stats = [r.ostat[h, mine_b]]
        for k in range(1, devices):
            stats.append(r.rstat[h, lax.rem(index + k, devices)])
        top = functools.reduce(jnp.maximum, [s[:1] for s in stats])
        factors = [jnp.exp2(s[:1] - top) for s in stats]
        total = functools.reduce(jnp.add, [s[1:2] * f for s, f in zip(stats, factors)])
        for k, f in enumerate(factors):
            r.gs[k : k + 1, :] = f / total
        r.gt[...] = r.gs[...].T
        col = r.gt[pl.ds(pl.multiple_of(far * (tz * group), 8), tz * group), :]
        value = r.oval[h, mine_b, far].astype(F32) * col[:, 0:1]
        for k in range(1, devices):
            got = r.rval[h, lax.rem(index + k, devices)].astype(F32)
            value = value + got * col[:, k : k + 1]
        r.agat[h, core, near, far] = value.astype(BF16).reshape(tz, group, HD)
        spread_out(*o_gather(h))

    def relay(h):
        pass_on(*o_gather(h), r.sh.at[h], r.rh.at[h])

    def mix(h):
        arrived(r.agat.at[h], r.sh.at[h], r.rh.at[h]).wait_recv()
        load_wo(h).wait()
        r.flat[...] = r.agat[h].reshape(qtok * group, HD).astype(F32)
        left = jnp.concatenate(
            [r.flat[pl.ds(j, qtok, stride=group), :].astype(BF16) for j in range(group)], axis=1
        )
        r.acc[...] += nn(left, r.wob[h])

    def middle(h):
        arrived(r.gat.at[h], r.sf.at[h], r.rf.at[h]).wait_recv()
        def between(b):
            if b == 1:
                @pl.when(h + 1 < kvh)
                def _():
                    stage_e(h + 1)

                @pl.when(h == kvh - 1)
                def _():
                    join(0)

        attend(h, between)

    def cached(h):
        for copy in load_cache(h):
            copy.wait()

    loop(kvh, cached)
    loop(kvh, middle)

    def tail(i):
        @pl.when(i < kvh - 1)
        def _():
            join(i + 1)

        @pl.when((i >= 2) & (i < kvh + 2))
        def _():
            relay(i - 2)

        @pl.when(i >= 3)
        def _():
            mix(i - 3)

    loop(kvh + 3, tail)
    r.out[...] = r.acc[...].astype(BF16)

    def drain(h):
        pair(h).wait_send()
        cross(h).wait_send()
        loop(half - 1, lambda i: long(h, i + 1).wait_send())
        for buf, send, recv in (q_gather(h), o_gather(h)):
            loop(chips - 1, lambda k: spreading(buf, send, recv, k + 1).wait_send())
        forward(r.gat.at[h], r.sf.at[h], r.rf.at[h]).wait_send()
        forward(r.agat.at[h], r.sh.at[h], r.rh.at[h]).wait_send()
        for b in range(blocks):
            def shipped(k):
                @pl.when(jnp.logical_not(is_me(b, k)))
                def _():
                    for copy in out_send(h, b, k):
                        copy.wait_send()

            loop(half, shipped)

    loop(kvh, drain)
    pair_kv().wait_send()
    cross_kv().wait_send()
    loop(half - 1, lambda i: long_kv(i + 1).wait_send())
    buf, send, recv = kv_gather()
    loop(chips - 1, lambda k: spreading(buf, send, recv, k + 1).wait_send())
    forward(r.gkv, r.ksf.at[0], r.krf.at[0]).wait_send()


def body(
    hidden, w_query, w_key, w_value, w_out, prefix_keys, prefix_values, key_scales, value_scales,
    demo_keys, demo_values, task_ids, demo_lengths, offsets,
):
    devices = lax.axis_size("seq")
    chips = devices // 2
    half = chips // SIDES
    qtok, depth = hidden.shape
    kvh = prefix_keys.shape[1] // HD
    group = w_query.shape[1] // HD // kvh
    tasks, demo_dev = demo_keys.shape[:2]
    pre_dev = prefix_keys.shape[0]
    tq = qtok // (2 * SIDES)
    tz = tq // half
    ku = 2 * kvh
    kuz = ku // half
    rows = tq * group
    cols = w_out.shape[1]
    cw = 4 * HD
    nch = group * HD // cw
    cfg = types.SimpleNamespace(
        kvh=kvh, group=group, half=half, devices=devices, tq=tq, tz=tz, qtok=qtok,
        blk=pre_dev // key_scales.shape[0], rows=rows, nch=nch, cw=cw, demo_dev=demo_dev,
        pre_dev=pre_dev, kuz=kuz,
    )
    smem = pl.BlockSpec(memory_space=pltpu.SMEM)
    hbm = pl.BlockSpec(memory_space=pltpu.HBM)
    ins = ["tasks", "lens", "offs", "ks", "vs"]
    ins += ["hid", "wq", "wk", "wv", "wo", "pk", "pv", "dk", "dv"]
    v = pltpu.VMEM

    def dma(*shape):
        return pltpu.SemaphoreType.DMA(shape)

    scratch = dict(
        hidb=v(hidden.shape, BF16), wkb=v(w_key.shape, BF16), wvb=v(w_value.shape, BF16),
        wqb=v((kvh * nch, depth, cw), BF16), wob=v((kvh, group * HD, cols), BF16),
        pkb=v((kvh, pre_dev, HD), BF16), pvb=v((kvh, pre_dev, HD), BF16),
        dkb=v((kvh, tasks, demo_dev, HD), BF16), dvb=v((kvh, tasks, demo_dev, HD), BF16),
        part=v((kvh, 2, SIDES, group, tq, HD), F32), recv1=v((kvh, SIDES, group, tq, HD), F32),
        own=v((kvh, group, tq, HD), F32), ysum=v((kvh, group, tq, HD), F32),
        yrecv=v((kvh, group, tq, HD), F32), zbuf=v((kvh, tq, group, HD), F32),
        zrecv=v((kvh, half - 1, tz, group, HD), F32),
        gat=v((kvh, 2, SIDES, half, tz, group, HD), BF16),
        kpart=v((2, SIDES, ku, tq, HD), F32), krecv1=v((SIDES, ku, tq, HD), F32),
        kown=v((ku, tq, HD), F32), kysum=v((ku, tq, HD), F32), kyrecv=v((ku, tq, HD), F32),
        kz=v((ku, tq, HD), F32), kzrecv=v((half - 1, kuz, tq, HD), F32),
        gkv=v((2, SIDES, half, kuz, tq, HD), BF16),
        scr0=v((rows, pre_dev), F32), scr1=v((rows, pre_dev), F32),
        wts0=v((rows, pre_dev), BF16), wts1=v((rows, pre_dev), BF16),
        dmask=v((qtok, demo_dev), F32), smask=v((qtok, qtok), F32),
        oval=v((kvh, 2 * SIDES, half, tz * group, HD), BF16),
        ostat=v((kvh, 2 * SIDES, STAT, rows), F32),
        rval=v((kvh, devices, tz * group, HD), BF16), rstat=v((kvh, devices, STAT, rows), F32),
        gs=v((HD, rows), F32), gt=v((rows, HD), F32),
        agat=v((kvh, 2, SIDES, half, tz, group, HD), BF16),
        flat=v((qtok * group, HD), F32), acc=v((qtok, cols), F32),
        s_in=dma(3), s_wq=dma(kvh * nch), s_wo=dma(kvh),
        s_pk=dma(kvh), s_pv=dma(kvh), s_dk=dma(kvh), s_dv=dma(kvh),
        s1=dma(kvh), r1=dma(kvh), sy=dma(kvh), ry=dma(kvh),
        sz=dma(kvh, half - 1), rz=dma(kvh, half - 1), sg=dma(kvh, chips), rg=dma(kvh, chips),
        sf=dma(kvh), rf=dma(kvh),
        ks1=dma(1), kr1=dma(1), ksy=dma(1), kry=dma(1), ksz=dma(half - 1), krz=dma(half - 1),
        ksg=dma(chips), krg=dma(chips), ksf=dma(1), krf=dma(1),
        so=dma(kvh, devices), ro=dma(kvh, devices), st=dma(kvh, devices), rt=dma(kvh, devices),
        sa=dma(kvh, chips), ra=dma(kvh, chips), sh=dma(kvh), rh=dma(kvh),
    )
    names = [*ins, "out", *scratch]

    def run(*refs):
        named = dict(zip(names, refs))
        named["scr"] = (named["scr0"], named["scr1"])
        named["wts"] = (named["wts0"], named["wts1"])
        kernel(cfg, list(named), *named.values())

    return pl.pallas_call(
        run,
        name="fused",
        out_shape=jax.ShapeDtypeStruct((qtok, cols), BF16),
        in_specs=[smem] * 5 + [hbm] * 9,
        out_specs=pl.BlockSpec(memory_space=pltpu.VMEM),
        scratch_shapes=list(scratch.values()),
        compiler_params=pltpu.CompilerParams(
            collective_id=0, has_side_effects=True, vmem_limit_bytes=63 << 20
        ),
    )(
        task_ids, demo_lengths, offsets, key_scales.T, value_scales.T,
        hidden, w_query, w_key, w_value, w_out,
        prefix_keys, prefix_values, demo_keys, demo_values,
    )


def solution(mesh):
    placed = (
        P("groups", "seq"),
        P("seq", None),
        P("seq", None),
        P("seq", None),
        P(None, "seq"),
        P(("groups", "seq"), None),
        P(("groups", "seq"), None),
        P(("groups", "seq"), None),
        P(("groups", "seq"), None),
        P("groups", "seq", None),
        P("groups", "seq", None),
        P("groups"),
        P("groups"),
        P("groups"),
    )
    return jax.shard_map(
        body, mesh=mesh, in_specs=placed, out_specs=P("groups", "seq"), check_vma=False
    )
```

time: 88.4 us -> 62.4 us (0.71)
  Pallas kernels: 84.1 us -> 60.7 us
  local copies, waits for them, and re-layouts: 3.96 us -> 1.47 us
    pallas_call x3 -> x1, Pallas kernels: 84.1 us -> 60.7 us  [body(): pl.pallas_call(run, name='fused', out_shape=jax.ShapeDtypeStruct((qtok, c...]
    unnamed x25 -> x1, local copies, waits for them, and re-layouts: 3.96 us -> 1.47 us
where the time goes in v1:
time: 62.4 us; the launch traced here: 62.2 us
  Pallas kernels  60.7 us (97%)
  local copies, waits for them, and re-layouts  1.47 us (2%)
    pallas_call x1, Pallas kernels, body(): pl.pallas_call(run, name='fused', out_shape=jax.ShapeDtypeStruct((qtok, c...  60.7 us
    unnamed x1, local copies, waits for them, and re-layouts  1.47 us

profile of v1, /device:TPU:0, one launch (start us, length us, event | category | flops | bytes accessed | tf_op | source)
XLA Modules:
  0.0 62.2 jit_solution(11369644394640390987)
XLA Ops:
  0.0 60.7 %fused.1 = bf16[32,1024]{1,0:T(8,128)(2,1)} custom-call(s32[32]{0:T(128)} %refs_0_.1, s32[16]{0:T(128)} %refs_1_.1, s32[32]{0:T(128)} %refs_2_.1, f32[4,16]{1,0:T(4,128)} %bitcast.2, f32[4,16]{1,0:T(4,128)} %bitcast.3, bf16[32,1024]{1,0:T(8,128)(2,1)} %refs_5_.1, bf16[1024,8192]{1,0:T(8,128)(2,1)} %refs_6_.1, bf16[1024,512]{1,0:T(8,128)(2,1)} %refs_7_.1, ...), custom_call_target="tpu_custom_call" | custom-call | tf_op jit(solution)/shard_map/fused/pallas_call | solution.py:593
  60.7 1.5 %copy.16 = bf16[32,1024]{1,0:T(8,128)(2,1)} copy(bf16[32,1024]{1,0:T(8,128)(2,1)} %fused.1) | data formatting | bytes 131072

commit v2 on v1

--- a/solution.py
+++ b/solution.py
@@ -78,10 +78,10 @@
     def load_cache(h):
         lanes = pl.ds(pl.multiple_of(h * HD, HD), HD)
         return (
-            pltpu.make_async_copy(r.pk.at[:, lanes], r.pkb.at[h], r.s_pk.at[h]),
-            pltpu.make_async_copy(r.dk.at[:, :, lanes], r.dkb.at[h], r.s_dk.at[h]),
-            pltpu.make_async_copy(r.pv.at[:, lanes], r.pvb.at[h], r.s_pv.at[h]),
-            pltpu.make_async_copy(r.dv.at[:, :, lanes], r.dvb.at[h], r.s_dv.at[h]),
+            pltpu.make_async_copy(r.pk.at[:, lanes], r.pkb.at[h], r.c_pk.at[h]),
+            pltpu.make_async_copy(r.dk.at[:, :, lanes], r.dkb.at[h], r.c_dk.at[h]),
+            pltpu.make_async_copy(r.pv.at[:, lanes], r.pvb.at[h], r.c_pv.at[h]),
+            pltpu.make_async_copy(r.dv.at[:, :, lanes], r.dvb.at[h], r.c_dv.at[h]),
         )
 
     small = [
@@ -96,15 +96,14 @@
 
     barrier = pltpu.get_barrier_semaphore()
 
-    def greet(k):
+    def hello(dev):
         pl.semaphore_signal(
-            barrier,
-            inc=1,
-            device_id={"seq": lax.rem(index + 1 + k, devices)},
-            device_id_type=pl.DeviceIdType.MESH,
-        )
-
-    loop(devices - 1, greet)
+            barrier, inc=1, device_id={"seq": dev}, device_id_type=pl.DeviceIdType.MESH
+        )
+
+    hello(partner)
+    hello(across)
+    loop(half - 1, lambda k: hello(device(up(k + 1), near, core)))
 
     lane_d = lax.broadcasted_iota(jnp.int32, (1, cfg.demo_dev), 1)
     lane_t = lax.broadcasted_iota(jnp.int32, (1, qtok), 1)
@@ -125,13 +124,12 @@
         r.smask[pl.ds(t, 1), :] = jnp.where(keep, 0.0, NEG)
 
     loop(qtok, mask)
-    r.gs[...] = jnp.zeros_like(r.gs)
     r.acc[...] = jnp.zeros_like(r.acc)
     small[0].wait()
 
-    def project(h):
+    def project(h, first, n_chunks):
         def chunk(n):
-            k = h * nch + n
+            k = h * nch + first + n
             load_wq(k).wait()
             res = nn(r.hidb[...], r.wqb[k])
             per = cw // HD
@@ -139,9 +137,10 @@
                 for s in range(SIDES):
                     at = (c * SIDES + s) * tq
                     for u in range(per):
-                        r.part[h, c, s, n * per + u] = res[at : at + tq, u * HD : (u + 1) * HD]
-
-        loop(nch, chunk)
+                        to = r.part.at[h, c, s, (first + n) * per + u]
+                        to[...] = res[at : at + tq, u * HD : (u + 1) * HD]
+
+        loop(n_chunks, chunk)
 
     def project_kv():
         for copy in small[1:]:
@@ -178,42 +177,53 @@
             r.ksz.at[i - 1], r.krz.at[i - 1], device(up(i), near, core),
         )
 
-    def side(k):
-        return lax.rem(near + lax.rem(k, 2), 2)
-
-    def spreading(buf, send, recv, k):
-        dev = device(up(k // 2), side(k), core)
-        piece = buf.at[core, near, far]
-        return remote(piece, piece, send.at[k], recv.at[k], dev)
-
-    def landing(buf, send, recv, k):
-        dev = device(up(k // 2), side(k), core)
-        piece = buf.at[core, side(k), down(k // 2)]
-        return remote(piece, piece, send.at[k], recv.at[k], dev)
-
-    def forward(buf, send, recv):
-        return remote(buf.at[core], buf.at[core], send, recv, partner)
-
-    def arrived(buf, send, recv):
-        return remote(buf.at[1 - core], buf.at[1 - core], send, recv, partner)
-
-    chips = SIDES * half
-
-    def spread_out(buf, send, recv):
-        loop(chips - 1, lambda k: spreading(buf, send, recv, k + 1).start())
-
-    def pass_on(buf, send, recv, fsend, frecv):
-        loop(chips - 1, lambda k: landing(buf, send, recv, k + 1).wait_recv())
-        forward(buf, fsend, frecv).start()
+    def spreading(g, i):
+        piece = g.buf.at[core, near, far]
+        return remote(piece, piece, g.sz.at[i], g.rz.at[i], device(up(i), near, core))
+
+    def landing(g, i):
+        piece = g.buf.at[core, near, down(i)]
+        return remote(piece, piece, g.sz.at[i], g.rz.at[i], device(up(i), near, core))
+
+    def crossing(g, n):
+        return remote(g.buf.at[core, n], g.buf.at[core, n], g.sy, g.ry, across)
+
+    def passing(g, c):
+        return remote(g.buf.at[c], g.buf.at[c], g.sp, g.rp, partner)
+
+    def gather_far(g):
+        loop(half - 1, lambda i: spreading(g, i + 1).start())
+
+    def gather_side(g):
+        loop(half - 1, lambda i: landing(g, i + 1).wait_recv())
+        crossing(g, near).start()
+
+    def gather_pair(g):
+        crossing(g, 1 - near).wait_recv()
+        passing(g, core).start()
+
+    def gather_end(g):
+        passing(g, 1 - core).wait_recv()
+
+    def gather_sent(g):
+        loop(half - 1, lambda i: spreading(g, i + 1).wait_send())
+        crossing(g, near).wait_send()
+        passing(g, core).wait_send()
+
+    def gather(buf, sems, h):
+        sz, rz, sy, ry, sp, rp = sems
+        return types.SimpleNamespace(
+            buf=buf, sz=sz.at[h], rz=rz.at[h], sy=sy.at[h], ry=ry.at[h], sp=sp.at[h], rp=rp.at[h]
+        )
 
     def q_gather(h):
-        return r.gat.at[h], r.sg.at[h], r.rg.at[h]
+        return gather(r.gat.at[h], (r.qsz, r.qrz, r.qsy, r.qry, r.qsp, r.qrp), h)
 
     def kv_gather():
-        return r.gkv, r.ksg, r.krg
+        return gather(r.gkv, (r.kgsz, r.kgrz, r.kgsy, r.kgry, r.kgsp, r.kgrp), 0)
 
     def o_gather(h):
-        return r.agat.at[h], r.sa.at[h], r.ra.at[h]
+        return gather(r.agat.at[h], (r.asz, r.arz, r.asy, r.ary, r.asp, r.arp), h)
 
     def stage_b(h):
         pair(h).wait_recv()
@@ -225,7 +235,7 @@
         pair_kv().wait_recv()
         r.kysum[...] = r.kpart[core, 1 - near] + r.krecv1[1 - near]
         cross_kv().start()
-        r.kown[...] = r.kpart[core, near] + r.krecv1[near]
+        r.kmine[...] = r.kpart[core, near] + r.krecv1[near]
 
     def stage_c(h):
         cross(h).wait_recv()
@@ -234,7 +244,7 @@
 
     def stage_c_kv():
         cross_kv().wait_recv()
-        r.kz[...] = r.kown[...] + r.kyrecv[...]
+        r.kz[...] = r.kmine[...] + r.kyrecv[...]
         loop(half - 1, lambda i: long_kv(i + 1).start())
 
     def stage_d(h):
@@ -243,7 +253,7 @@
             long(h, i).wait_recv()
             total = total + r.zrecv[h, i - 1]
         r.gat[h, core, near, far] = total.astype(BF16)
-        spread_out(*q_gather(h))
+        gather_far(q_gather(h))
 
     def stage_d_kv():
         total = r.kz[pl.ds(far * cfg.kuz, cfg.kuz)]
@@ -251,86 +261,98 @@
             long_kv(i).wait_recv()
             total = total + r.kzrecv[i - 1]
         r.gkv[core, near, far] = total.astype(BF16)
-        spread_out(*kv_gather())
-
-    def stage_e(h):
-        pass_on(*q_gather(h), r.sf.at[h], r.rf.at[h])
-
-    def front(i):
-        @pl.when(i < kvh)
-        def _():
-            project(i)
-            pair(i).start()
-
-        @pl.when(i < kvh + 1)
-        def _():
-            stage_b(i - 1)
-
-        @pl.when(i == 1)
-        def _():
-            stage_b_kv()
-
-        @pl.when((i >= 3) & (i < kvh + 3))
-        def _():
-            stage_c(i - 3)
-
-        @pl.when(i == 3)
-        def _():
-            stage_c_kv()
-
-            def caches(h):
-                for copy in load_cache(h):
-                    copy.start()
-
-            loop(kvh, caches)
-            loop(kvh, lambda h: load_wo(h).start())
-
-        @pl.when(i >= 5)
-        def _():
-            stage_d(i - 5)
-
-        @pl.when(i == 5)
-        def _():
-            stage_d_kv()
-
-    project(0)
-    pl.semaphore_wait(barrier, devices - 1)
-    pair(0).start()
-    project_kv()
-    pair_kv().start()
-    loop(kvh + 4, lambda i: front(i + 1))
-    stage_e(0)
-    pass_on(*kv_gather(), r.ksf.at[0], r.krf.at[0])
-    arrived(r.gkv, r.ksf.at[0], r.krf.at[0]).wait_recv()
-
-    def out_send(h, b, k):
-        c, s = b // SIDES, b % SIDES
-        dev = device(up(k), s, c)
+        gather_far(kv_gather())
+
+    first_row = lax.broadcasted_iota(jnp.int32, (STAT, rows), 0)
+
+    def send_pair(h):
+        to = (r.s_pv.at[h], r.r_pv.at[h]), (r.s_ps.at[h], r.r_ps.at[h])
+        return (
+            remote(r.pval.at[h, 1 - core], r.pgot.at[h], *to[0], partner),
+            remote(r.pstat.at[h, 1 - core], r.pgots.at[h], *to[1], partner),
+        )
+
+    def send_side(h):
+        return (
+            remote(r.yval.at[h], r.ygot.at[h], r.s_yv.at[h], r.r_yv.at[h], across),
+            remote(r.ystat.at[h], r.ygots.at[h], r.s_ys.at[h], r.r_ys.at[h], across),
+        )
+
+    def send_far(h, i):
+        dev = device(up(i), near, core)
+        k = i - 1
         return (
             remote(
-                r.oval.at[h, b, up(k)], r.rval.at[h, index],
-                r.so.at[h, b * half + k], r.ro.at[h, index], dev,
+                r.zval.at[h, up(i)], r.zgot.at[h, k], r.s_zv.at[h, k], r.r_zv.at[h, k], dev
             ),
             remote(
-                r.ostat.at[h, b], r.rstat.at[h, index],
-                r.st.at[h, b * half + k], r.rt.at[h, index], dev,
+                r.kstat.at[h], r.zgots.at[h, k], r.s_zs.at[h, k], r.r_zs.at[h, k], dev
             ),
         )
 
-    def is_me(b, k):
-        return (k == 0) & (core == b // SIDES) & (near == b % SIDES)
-
-    def out_from(h, dev):
-        return (
-            remote(r.oval.at[h, 0, 0], r.rval.at[h, dev], r.so.at[h, 0], r.ro.at[h, dev], dev),
-            remote(r.ostat.at[h, 0], r.rstat.at[h, dev], r.st.at[h, 0], r.rt.at[h, dev], dev),
-        )
+    def start(copies):
+        for copy in copies:
+            copy.start()
+
+    def receive(copies):
+        for copy in copies:
+            copy.wait_recv()
+
+    def sent(copies):
+        for copy in copies:
+            copy.wait_send()
+
+    def join(a, a_stat, b, b_stat):
+        top = jnp.maximum(a_stat[:1], b_stat[:1])
+        fa, fb = jnp.exp2(a_stat[:1] - top), jnp.exp2(b_stat[:1] - top)
+        stat = jnp.where(first_row == 0, top, a_stat * fa + b_stat * fb)
+        col = jnp.where(first_row == 0, fa, fb).T
+        return a * col[:, 0:1] + b.astype(F32) * col[:, 1:2], stat
+
+    def merge_pair(h):
+        receive(send_pair(h))
+
+        def both(n):
+            return join(r.pval[h, core, n], r.pstat[h, core, n], r.pgot[h, n], r.pgots[h, n])
+
+        value, stat = both(1 - near)
+        r.yval[h] = value.astype(BF16)
+        r.ystat[h] = stat
+        start(send_side(h))
+        r.kval[h], r.kown[h] = both(near)
+
+    def merge_side(h):
+        receive(send_side(h))
+        value, stat = join(r.kval[h], r.kown[h], r.ygot[h], r.ygots[h])
+        r.zval[h] = value.astype(BF16).reshape(half, tz * group, HD)
+        r.kstat[h] = stat
+        loop(half - 1, lambda i: start(send_far(h, i + 1)))
+        r.kval[h] = value
+
+    def merge_far(h):
+        loop(half - 1, lambda i: receive(send_far(h, i + 1)))
+        stats = [r.kstat[h], *[r.zgots[h, k] for k in range(half - 1)]]
+        top = functools.reduce(jnp.maximum, [s[:1] for s in stats])
+        factors = [jnp.exp2(s[:1] - top) for s in stats]
+        total = functools.reduce(jnp.add, [s[1:2] * f for s, f in zip(stats, factors)])
+        table = jnp.zeros((STAT, rows), F32)
+        for k, f in enumerate(factors):
+            table = jnp.where(first_row == k, f / total, table)
+        r.gt[...] = table.T
+        deep = tz * group
+        here = pl.ds(pl.multiple_of(far * deep, 8), deep)
+        col = r.gt[here, :]
+        value = r.kval[h, here, :] * col[:, 0:1]
+        for k in range(1, half):
+            value = value + r.zgot[h, k - 1].astype(F32) * col[:, k : k + 1]
+        r.agat[h, core, near, far] = value.astype(BF16).reshape(tz, group, HD)
+        gather_far(o_gather(h))
 
     width = 2 * blk
     steps = cfg.pre_dev // width
     blocks = 2 * SIDES
 
-    def attend(h, between):
+    def attend(h):
         def query(b):
             return r.gat[h, b // SIDES, b % SIDES].reshape(rows, HD)
 
@@ -404,47 +426,14 @@
                 axis=0,
             )
             lane = lax.broadcasted_iota(jnp.int32, (rows, HD), 1)
-            r.ostat[h, b] = jnp.where(lane == 0, top, total).T[:STAT]
-            r.oval[h, b] = value.astype(BF16).reshape(half, tz * group, HD)
-
-            def ship(k):
-                @pl.when(jnp.logical_not(is_me(b, k)))
-                def _():
-                    for copy in out_send(h, b, k):
-                        copy.start()
-
-            loop(half, ship)
-            between(b)
-
-    def join(h):
-        def take(k):
-            for copy in out_from(h, lax.rem(index + 1 + k, devices)):
-                copy.wait_recv()
-
-        loop(devices - 1, take)
-        mine_b = core * SIDES + near
-        stats = [r.ostat[h, mine_b]]
-        for k in range(1, devices):
-            stats.append(r.rstat[h, lax.rem(index + k, devices)])
-        top = functools.reduce(jnp.maximum, [s[:1] for s in stats])
-        factors = [jnp.exp2(s[:1] - top) for s in stats]
-        total = functools.reduce(jnp.add, [s[1:2] * f for s, f in zip(stats, factors)])
-        for k, f in enumerate(factors):
-            r.gs[k : k + 1, :] = f / total
-        r.gt[...] = r.gs[...].T
-        col = r.gt[pl.ds(pl.multiple_of(far * (tz * group), 8), tz * group), :]
-        value = r.oval[h, mine_b, far].astype(F32) * col[:, 0:1]
-        for k in range(1, devices):
-            got = r.rval[h, lax.rem(index + k, devices)].astype(F32)
-            value = value + got * col[:, k : k + 1]
-        r.agat[h, core, near, far] = value.astype(BF16).reshape(tz, group, HD)
-        spread_out(*o_gather(h))
-
-    def relay(h):
-        pass_on(*o_gather(h), r.sh.at[h], r.rh.at[h])
+            c, n = b // SIDES, b % SIDES
+            r.pstat[h, c, n] = jnp.where(lane == 0, top, total).T[:STAT]
+            r.pval[h, c, n] = value
+
+        start(send_pair(h))
 
     def mix(h):
-        arrived(r.agat.at[h], r.sh.at[h], r.rh.at[h]).wait_recv()
+        gather_end(o_gather(h))
         load_wo(h).wait()
         r.flat[...] = r.agat[h].reshape(qtok * group, HD).astype(F32)
         left = jnp.concatenate(
@@ -452,67 +441,86 @@
         )
         r.acc[...] += nn(left, r.wob[h])
 
-    def middle(h):
-        arrived(r.gat.at[h], r.sf.at[h], r.rf.at[h]).wait_recv()
-        def between(b):
-            if b == 1:
-                @pl.when(h + 1 < kvh)
-                def _():
-                    stage_e(h + 1)
-
-                @pl.when(h == kvh - 1)
-                def _():
-                    join(0)
-
-        attend(h, between)
-
     def cached(h):
         for copy in load_cache(h):
             copy.wait()
 
-    loop(kvh, cached)
-    loop(kvh, middle)
-
-    def tail(i):
-        @pl.when(i < kvh - 1)
+    def rest(h):
+        for copy in load_cache(h):
+            copy.start()
+
+    def later(h):
+        load_wo(h).start()
+
+    half_way = nch // 2
+
+    def project_start(h):
+        project(h, 0, half_way)
+
+    def project_end(h):
+        project(h, half_way, nch - half_way)
+        pair(h).start()
+
+        @pl.when(h == kvh - 1)
         def _():
-            join(i + 1)
-
-        @pl.when((i >= 2) & (i < kvh + 2))
-        def _():
-            relay(i - 2)
-
-        @pl.when(i >= 3)
-        def _():
-            mix(i - 3)
-
-    loop(kvh + 3, tail)
+            loop(kvh, rest)
+            loop(kvh, later)
+
+    def ready():
+        loop(kvh, cached)
+        gather_end(kv_gather())
+
+    def turn(h):
+        gather_end(q_gather(h))
+        attend(h)
+
+    stages = (
+        (12, merge_side, None),
+        (0, project_start, None),
+        (1, stage_b, stage_b_kv),
+        (0, project_end, None),
+        (5, stage_d, stage_d_kv),
+        (9, turn, ready),
+        (7, lambda h: gather_side(q_gather(h)), lambda: gather_side(kv_gather())),
+        (2, stage_c, stage_c_kv),
+        (14, merge_far, None),
+        (8, lambda h: gather_pair(q_gather(h)), lambda: gather_pair(kv_gather())),
+        (16, lambda h: gather_side(o_gather(h)), None),
+        (18, mix, None),
+        (10, merge_pair, None),
+        (17, lambda h: gather_pair(o_gather(h)), None),
+    )
+
+    def step(at):
+        i = at + 1
+        for late, stage, extra in stages:
+            if extra is not None:
+                pl.when(i == late)(extra)
+            pl.when((i >= late) & (i < late + kvh))(functools.partial(stage, i - late))
+
+    project(0, 0, nch)
+    pl.semaphore_wait(barrier, 2 + half - 1)
+    pair(0).start()
+    project_kv()
+    pair_kv().start()
+    loop(kvh + 17, step)
     r.out[...] = r.acc[...].astype(BF16)
 
     def drain(h):
         pair(h).wait_send()
         cross(h).wait_send()
         loop(half - 1, lambda i: long(h, i + 1).wait_send())
-        for buf, send, recv in (q_gather(h), o_gather(h)):
-            loop(chips - 1, lambda k: spreading(buf, send, recv, k + 1).wait_send())
-        forward(r.gat.at[h], r.sf.at[h], r.rf.at[h]).wait_send()
-        forward(r.agat.at[h], r.sh.at[h], r.rh.at[h]).wait_send()
-        for b in range(blocks):
-            def shipped(k):
-                @pl.when(jnp.logical_not(is_me(b, k)))
-                def _():
-                    for copy in out_send(h, b, k):
-                        copy.wait_send()
-
-            loop(half, shipped)
+        gather_sent(q_gather(h))
+        gather_sent(o_gather(h))
+        sent(send_pair(h))
+        sent(send_side(h))
+        loop(half - 1, lambda i: sent(send_far(h, i + 1)))
 
     loop(kvh, drain)
     pair_kv().wait_send()
     cross_kv().wait_send()
     loop(half - 1, lambda i: long_kv(i + 1).wait_send())
-    buf, send, recv = kv_gather()
-    loop(chips - 1, lambda k: spreading(buf, send, recv, k + 1).wait_send())
-    forward(r.gkv, r.ksf.at[0], r.krf.at[0]).wait_send()
+    gather_sent(kv_gather())
 
 
 def body(
@@ -560,27 +568,35 @@
         zrecv=v((kvh, half - 1, tz, group, HD), F32),
         gat=v((kvh, 2, SIDES, half, tz, group, HD), BF16),
         kpart=v((2, SIDES, ku, tq, HD), F32), krecv1=v((SIDES, ku, tq, HD), F32),
-        kown=v((ku, tq, HD), F32), kysum=v((ku, tq, HD), F32), kyrecv=v((ku, tq, HD), F32),
+        kmine=v((ku, tq, HD), F32), kysum=v((ku, tq, HD), F32), kyrecv=v((ku, tq, HD), F32),
         kz=v((ku, tq, HD), F32), kzrecv=v((half - 1, kuz, tq, HD), F32),
         gkv=v((2, SIDES, half, kuz, tq, HD), BF16),
         scr0=v((rows, pre_dev), F32), scr1=v((rows, pre_dev), F32),
         wts0=v((rows, pre_dev), BF16), wts1=v((rows, pre_dev), BF16),
         dmask=v((qtok, demo_dev), F32), smask=v((qtok, qtok), F32),
-        oval=v((kvh, 2 * SIDES, half, tz * group, HD), BF16),
-        ostat=v((kvh, 2 * SIDES, STAT, rows), F32),
-        rval=v((kvh, devices, tz * group, HD), BF16), rstat=v((kvh, devices, STAT, rows), F32),
-        gs=v((HD, rows), F32), gt=v((rows, HD), F32),
+        pval=v((kvh, 2, SIDES, rows, HD), F32), pstat=v((kvh, 2, SIDES, STAT, rows), F32),
+        pgot=v((kvh, SIDES, rows, HD), F32), pgots=v((kvh, SIDES, STAT, rows), F32),
+        yval=v((kvh, rows, HD), BF16), ystat=v((kvh, STAT, rows), F32),
+        ygot=v((kvh, rows, HD), BF16), ygots=v((kvh, STAT, rows), F32),
+        kval=v((kvh, rows, HD), F32), kown=v((kvh, STAT, rows), F32),
+        kstat=v((kvh, STAT, rows), F32), zval=v((kvh, half, tz * group, HD), BF16),
+        zgot=v((kvh, half - 1, tz * group, HD), BF16), zgots=v((kvh, half - 1, STAT, rows), F32),
+        gt=v((rows, STAT), F32),
         agat=v((kvh, 2, SIDES, half, tz, group, HD), BF16),
         flat=v((qtok * group, HD), F32), acc=v((qtok, cols), F32),
         s_in=dma(3), s_wq=dma(kvh * nch), s_wo=dma(kvh),
-        s_pk=dma(kvh), s_pv=dma(kvh), s_dk=dma(kvh), s_dv=dma(kvh),
+        c_pk=dma(kvh), c_pv=dma(kvh), c_dk=dma(kvh), c_dv=dma(kvh),
         s1=dma(kvh), r1=dma(kvh), sy=dma(kvh), ry=dma(kvh),
-        sz=dma(kvh, half - 1), rz=dma(kvh, half - 1), sg=dma(kvh, chips), rg=dma(kvh, chips),
-        sf=dma(kvh), rf=dma(kvh),
+        sz=dma(kvh, half - 1), rz=dma(kvh, half - 1),
         ks1=dma(1), kr1=dma(1), ksy=dma(1), kry=dma(1), ksz=dma(half - 1), krz=dma(half - 1),
-        ksg=dma(chips), krg=dma(chips), ksf=dma(1), krf=dma(1),
-        so=dma(kvh, devices), ro=dma(kvh, devices), st=dma(kvh, devices), rt=dma(kvh, devices),
-        sa=dma(kvh, chips), ra=dma(kvh, chips), sh=dma(kvh), rh=dma(kvh),
+        **{
+            f"{g}{d}{e}": dma(n, half) if e == "z" else dma(n)
+            for g, n in (("q", kvh), ("kg", 1), ("a", kvh))
+            for d in "sr"
+            for e in "zyp"
+        },
+        **{f"{d}_{e}": dma(kvh) for d in "sr" for e in ("pv", "ps", "yv", "ys")},
+        **{f"{d}_{e}": dma(kvh, half - 1) for d in "sr" for e in ("zv", "zs")},
     )
     names = [*ins, "out", *scratch]
 

time: 62.4 us -> 65.4 us (1.048)
  Pallas kernels: 60.7 us -> 63.8 us
    pallas_call x1, Pallas kernels: 60.7 us -> 63.8 us  [body(): pl.pallas_call(run, name='fused', out_shape=jax.ShapeDtypeStruct((qtok, c...]
where the time goes in v2:
time: 65.4 us; the launch traced here: 65.3 us
  Pallas kernels  63.8 us (98%)
  local copies, waits for them, and re-layouts  1.47 us (2%)
    pallas_call x1, Pallas kernels, body(): pl.pallas_call(run, name='fused', out_shape=jax.ShapeDtypeStruct((qtok, c...  63.8 us
    unnamed x1, local copies, waits for them, and re-layouts  1.47 us

profile of v2, /device:TPU:0, one launch (start us, length us, event | category | flops | bytes accessed | tf_op | source)
XLA Modules:
  0.0 65.3 jit_solution(10151501703552126290)
XLA Ops:
  0.0 63.8 %fused.1 = bf16[32,1024]{1,0:T(8,128)(2,1)} custom-call(s32[32]{0:T(128)} %refs_0_.1, s32[16]{0:T(128)} %refs_1_.1, s32[32]{0:T(128)} %refs_2_.1, f32[4,16]{1,0:T(4,128)} %bitcast.2, f32[4,16]{1,0:T(4,128)} %bitcast.3, bf16[32,1024]{1,0:T(8,128)(2,1)} %refs_5_.1, bf16[1024,8192]{1,0:T(8,128)(2,1)} %refs_6_.1, bf16[1024,512]{1,0:T(8,128)(2,1)} %refs_7_.1, ...), custom_call_target="tpu_custom_call" | custom-call | tf_op jit(solution)/shard_map/fused/pallas_call | solution.py:609
  63.8 1.5 %copy.16 = bf16[32,1024]{1,0:T(8,128)(2,1)} copy(bf16[32,1024]{1,0:T(8,128)(2,1)} %fused.1) | data formatting | bytes 131072

commit v3 on v1

--- a/solution.py
+++ b/solution.py
@@ -78,10 +78,10 @@
     def load_cache(h):
         lanes = pl.ds(pl.multiple_of(h * HD, HD), HD)
         return (
-            pltpu.make_async_copy(r.pk.at[:, lanes], r.pkb.at[h], r.s_pk.at[h]),
-            pltpu.make_async_copy(r.dk.at[:, :, lanes], r.dkb.at[h], r.s_dk.at[h]),
-            pltpu.make_async_copy(r.pv.at[:, lanes], r.pvb.at[h], r.s_pv.at[h]),
-            pltpu.make_async_copy(r.dv.at[:, :, lanes], r.dvb.at[h], r.s_dv.at[h]),
+            pltpu.make_async_copy(r.pk.at[:, lanes], r.pkb.at[h], r.c_pk.at[h]),
+            pltpu.make_async_copy(r.dk.at[:, :, lanes], r.dkb.at[h], r.c_dk.at[h]),
+            pltpu.make_async_copy(r.pv.at[:, lanes], r.pvb.at[h], r.c_pv.at[h]),
+            pltpu.make_async_copy(r.dv.at[:, :, lanes], r.dvb.at[h], r.c_dv.at[h]),
         )
 
     small = [
@@ -96,15 +96,24 @@
 
     barrier = pltpu.get_barrier_semaphore()
 
-    def greet(k):
+    def hello(dev):
         pl.semaphore_signal(
-            barrier,
-            inc=1,
-            device_id={"seq": lax.rem(index + 1 + k, devices)},
-            device_id_type=pl.DeviceIdType.MESH,
+            barrier, inc=1, device_id={"seq": dev}, device_id_type=pl.DeviceIdType.MESH
         )
 
-    loop(devices - 1, greet)
+    hello(partner)
+    chips = SIDES * half
+
+    def side(k):
+        return lax.rem(near + lax.rem(k, 2), 2)
+
+    def chip_at(k):
+        return device(up(k // 2), side(k), core)
+
+    def chip_from(k):
+        return down(k // 2), side(k)
+
+    loop(chips - 1, lambda k: hello(chip_at(k + 1)))
 
     lane_d = lax.broadcasted_iota(jnp.int32, (1, cfg.demo_dev), 1)
     lane_t = lax.broadcasted_iota(jnp.int32, (1, qtok), 1)
@@ -125,7 +134,6 @@
         r.smask[pl.ds(t, 1), :] = jnp.where(keep, 0.0, NEG)
 
     loop(qtok, mask)
-    r.gs[...] = jnp.zeros_like(r.gs)
     r.acc[...] = jnp.zeros_like(r.acc)
     small[0].wait()
 
@@ -178,26 +186,19 @@
             r.ksz.at[i - 1], r.krz.at[i - 1], device(up(i), near, core),
         )
 
-    def side(k):
-        return lax.rem(near + lax.rem(k, 2), 2)
-
     def spreading(buf, send, recv, k):
-        dev = device(up(k // 2), side(k), core)
         piece = buf.at[core, near, far]
-        return remote(piece, piece, send.at[k], recv.at[k], dev)
+        return remote(piece, piece, send.at[k], recv.at[k], chip_at(k))
 
     def landing(buf, send, recv, k):
-        dev = device(up(k // 2), side(k), core)
         piece = buf.at[core, side(k), down(k // 2)]
-        return remote(piece, piece, send.at[k], recv.at[k], dev)
+        return remote(piece, piece, send.at[k], recv.at[k], chip_at(k))
 
     def forward(buf, send, recv):
         return remote(buf.at[core], buf.at[core], send, recv, partner)
 
     def arrived(buf, send, recv):
         return remote(buf.at[1 - core], buf.at[1 - core], send, recv, partner)
-
-    chips = SIDES * half
 
     def spread_out(buf, send, recv):
         loop(chips - 1, lambda k: spreading(buf, send, recv, k + 1).start())
@@ -294,7 +295,7 @@
             stage_d_kv()
 
     project(0)
-    pl.semaphore_wait(barrier, devices - 1)
+    pl.semaphore_wait(barrier, chips)
     pair(0).start()
     project_kv()
     pair_kv().start()
@@ -303,28 +304,74 @@
     pass_on(*kv_gather(), r.ksf.at[0], r.krf.at[0])
     arrived(r.gkv, r.ksf.at[0], r.krf.at[0]).wait_recv()
 
-    def out_send(h, b, k):
-        c, s = b // SIDES, b % SIDES
-        dev = device(up(k), s, c)
+    first_row = lax.broadcasted_iota(jnp.int32, (STAT, rows), 0) == 0
+    deep = tz * group
+
+    def send_pair(h):
         return (
             remote(
-                r.oval.at[h, b, up(k)], r.rval.at[h, index],
-                r.so.at[h, b * half + k], r.ro.at[h, index], dev,
+                r.pval.at[h, 1 - core], r.pgot.at[h], r.s_pv.at[h], r.r_pv.at[h], partner
             ),
             remote(
-                r.ostat.at[h, b], r.rstat.at[h, index],
-                r.st.at[h, b * half + k], r.rt.at[h, index], dev,
+                r.pstat.at[h, 1 - core], r.pgots.at[h], r.s_ps.at[h], r.r_ps.at[h], partner
             ),
         )
 
-    def is_me(b, k):
-        return (k == 0) & (core == b // SIDES) & (near == b % SIDES)
-
-    def out_from(h, dev):
+    def send_own(h, k):
         return (
-            remote(r.oval.at[h, 0, 0], r.rval.at[h, dev], r.so.at[h, 0], r.ro.at[h, dev], dev),
-            remote(r.ostat.at[h, 0], r.rstat.at[h, dev], r.st.at[h, 0], r.rt.at[h, dev], dev),
+            remote(
+                r.oval.at[h, side(k), up(k // 2)], r.ogot.at[h, k],
+                r.s_ov.at[h, k], r.r_ov.at[h, k], chip_at(k),
+            ),
+            remote(
+                r.ostat.at[h, side(k)], r.ogots.at[h, k],
+                r.s_os.at[h, k], r.r_os.at[h, k], chip_at(k),
+            ),
         )
+
+    def start(copies):
+        for copy in copies:
+            copy.start()
+
+    def receive(copies):
+        for copy in copies:
+            copy.wait_recv()
+
+    def sent(copies):
+        for copy in copies:
+            copy.wait_send()
+
+    def merge_pair(h):
+        receive(send_pair(h))
+        for n in range(SIDES):
+            a, b = r.pstat[h, core, n], r.pgots[h, n]
+            top = jnp.maximum(a[:1], b[:1])
+            fa, fb = jnp.exp2(a[:1] - top), jnp.exp2(b[:1] - top)
+            stat = jnp.where(first_row, top, a * fa + b * fb)
+            col = jnp.where(first_row, fa, fb).T
+            value = r.pval[h, core, n] * col[:, 0:1] + r.pgot[h, n] * col[:, 1:2]
+            r.oval[h, n] = value.astype(BF16).reshape(half, deep, HD)
+            r.ostat[h, n] = stat[:2]
+        loop(chips - 1, lambda k: start(send_own(h, k + 1)))
+
+    def merge_own(h):
+        loop(chips - 1, lambda k: receive(send_own(h, k + 1)))
+        stats = [r.ostat[h, near], *[r.ogots[h, k] for k in range(1, chips)]]
+        top = functools.reduce(jnp.maximum, [s[:1] for s in stats])
+        factors = [jnp.exp2(s[:1] - top) for s in stats]
+        total = functools.reduce(jnp.add, [s[1:2] * f for s, f in zip(stats, factors)])
+        depth = r.gt.shape[1]
+        row = lax.broadcasted_iota(jnp.int32, (depth, rows), 0)
+        table = jnp.zeros((depth, rows), F32)
+        for k, f in enumerate(factors):
+            table = jnp.where(row == k, f / total, table)
+        r.gt[...] = table.T
+        col = r.gt[pl.ds(pl.multiple_of(far * deep, 8), deep), :]
+        value = r.oval[h, near, far].astype(F32) * col[:, 0:1]
+        for k in range(1, chips):
+            value = value + r.ogot[h, k].astype(F32) * col[:, k : k + 1]
+        r.agat[h, core, near, far] = value.astype(BF16).reshape(tz, group, HD)
+        spread_out(*o_gather(h))
 
     width = 2 * blk
     steps = cfg.pre_dev // width
@@ -404,41 +451,12 @@
                 axis=0,
             )
             lane = lax.broadcasted_iota(jnp.int32, (rows, HD), 1)
-            r.ostat[h, b] = jnp.where(lane == 0, top, total).T[:STAT]
-            r.oval[h, b] = value.astype(BF16).reshape(half, tz * group, HD)
-
-            def ship(k):
-                @pl.when(jnp.logical_not(is_me(b, k)))
-                def _():
-                    for copy in out_send(h, b, k):
-                        copy.start()
-
-            loop(half, ship)
+            c, n = b // SIDES, b % SIDES
+            r.pstat[h, c, n] = jnp.where(lane == 0, top, total).T[:STAT]
+            r.pval[h, c, n] = value
             between(b)
 
-    def join(h):
-        def take(k):
-            for copy in out_from(h, lax.rem(index + 1 + k, devices)):
-                copy.wait_recv()
-
-        loop(devices - 1, take)
-        mine_b = core * SIDES + near
-        stats = [r.ostat[h, mine_b]]
-        for k in range(1, devices):
-            stats.append(r.rstat[h, lax.rem(index + k, devices)])
-        top = functools.reduce(jnp.maximum, [s[:1] for s in stats])
-        factors = [jnp.exp2(s[:1] - top) for s in stats]
-        total = functools.reduce(jnp.add, [s[1:2] * f for s, f in zip(stats, factors)])
-        for k, f in enumerate(factors):
-            r.gs[k : k + 1, :] = f / total
-        r.gt[...] = r.gs[...].T
-        col = r.gt[pl.ds(pl.multiple_of(far * (tz * group), 8), tz * group), :]
-        value = r.oval[h, mine_b, far].astype(F32) * col[:, 0:1]
-        for k in range(1, devices):
-            got = r.rval[h, lax.rem(index + k, devices)].astype(F32)
-            value = value + got * col[:, k : k + 1]
-        r.agat[h, core, near, far] = value.astype(BF16).reshape(tz, group, HD)
-        spread_out(*o_gather(h))
+        start(send_pair(h))
 
     def relay(h):
         pass_on(*o_gather(h), r.sh.at[h], r.rh.at[h])
@@ -455,14 +473,20 @@
     def middle(h):
         arrived(r.gat.at[h], r.sf.at[h], r.rf.at[h]).wait_recv()
         def between(b):
+            if b == 0:
+                @pl.when(h > 0)
+                def _():
+                    merge_pair(h - 1)
+
             if b == 1:
                 @pl.when(h + 1 < kvh)
                 def _():
                     stage_e(h + 1)
 
+            if b == 2:
                 @pl.when(h == kvh - 1)
                 def _():
-                    join(0)
+                    merge_own(0)
 
         attend(h, between)
 
@@ -472,21 +496,26 @@
 
     loop(kvh, cached)
     loop(kvh, middle)
+    merge_pair(kvh - 1)
 
     def tail(i):
-        @pl.when(i < kvh - 1)
-        def _():
-            join(i + 1)
-
-        @pl.when((i >= 2) & (i < kvh + 2))
-        def _():
-            relay(i - 2)
-
-        @pl.when(i >= 3)
-        def _():
-            mix(i - 3)
-
-    loop(kvh + 3, tail)
+        @pl.when((i >= 2) & (i < kvh))
+        def _():
+            merge_own(i - 1)
+
+        @pl.when((i >= 3) & (i < kvh + 3))
+        def _():
+            relay(i - 3)
+
+        @pl.when(i == 3)
+        def _():
+            merge_own(kvh - 1)
+
+        @pl.when(i >= 4)
+        def _():
+            mix(i - 4)
+
+    loop(kvh + 4, tail)
     r.out[...] = r.acc[...].astype(BF16)
 
     def drain(h):
@@ -497,14 +526,8 @@
             loop(chips - 1, lambda k: spreading(buf, send, recv, k + 1).wait_send())
         forward(r.gat.at[h], r.sf.at[h], r.rf.at[h]).wait_send()
         forward(r.agat.at[h], r.sh.at[h], r.rh.at[h]).wait_send()
-        for b in range(blocks):
-            def shipped(k):
-                @pl.when(jnp.logical_not(is_me(b, k)))
-                def _():
-                    for copy in out_send(h, b, k):
-                        copy.wait_send()
-
-            loop(half, shipped)
+        sent(send_pair(h))
+        loop(chips - 1, lambda k: sent(send_own(h, k + 1)))
 
     loop(kvh, drain)
     pair_kv().wait_send()
@@ -566,20 +589,22 @@
         scr0=v((rows, pre_dev), F32), scr1=v((rows, pre_dev), F32),
         wts0=v((rows, pre_dev), BF16), wts1=v((rows, pre_dev), BF16),
         dmask=v((qtok, demo_dev), F32), smask=v((qtok, qtok), F32),
-        oval=v((kvh, 2 * SIDES, half, tz * group, HD), BF16),
-        ostat=v((kvh, 2 * SIDES, STAT, rows), F32),
-        rval=v((kvh, devices, tz * group, HD), BF16), rstat=v((kvh, devices, STAT, rows), F32),
-        gs=v((HD, rows), F32), gt=v((rows, HD), F32),
+        pval=v((kvh, 2, SIDES, rows, HD), F32), pstat=v((kvh, 2, SIDES, STAT, rows), F32),
+        pgot=v((kvh, SIDES, rows, HD), F32), pgots=v((kvh, SIDES, STAT, rows), F32),
+        oval=v((kvh, SIDES, half, tz * group, HD), BF16), ostat=v((kvh, SIDES, 2, rows), F32),
+        ogot=v((kvh, chips, tz * group, HD), BF16), ogots=v((kvh, chips, 2, rows), F32),
+        gt=v((rows, max(STAT, chips)), F32),
         agat=v((kvh, 2, SIDES, half, tz, group, HD), BF16),
         flat=v((qtok * group, HD), F32), acc=v((qtok, cols), F32),
         s_in=dma(3), s_wq=dma(kvh * nch), s_wo=dma(kvh),
-        s_pk=dma(kvh), s_pv=dma(kvh), s_dk=dma(kvh), s_dv=dma(kvh),
+        c_pk=dma(kvh), c_pv=dma(kvh), c_dk=dma(kvh), c_dv=dma(kvh),
         s1=dma(kvh), r1=dma(kvh), sy=dma(kvh), ry=dma(kvh),
         sz=dma(kvh, half - 1), rz=dma(kvh, half - 1), sg=dma(kvh, chips), rg=dma(kvh, chips),
         sf=dma(kvh), rf=dma(kvh),
         ks1=dma(1), kr1=dma(1), ksy=dma(1), kry=dma(1), ksz=dma(half - 1), krz=dma(half - 1),
         ksg=dma(chips), krg=dma(chips), ksf=dma(1), krf=dma(1),
-        so=dma(kvh, devices), ro=dma(kvh, devices), st=dma(kvh, devices), rt=dma(kvh, devices),
+        **{f"{d}_{e}": dma(kvh) for d in "sr" for e in ("pv", "ps")},
+        **{f"{d}_{e}": dma(kvh, chips) for d in "sr" for e in ("ov", "os")},
         sa=dma(kvh, chips), ra=dma(kvh, chips), sh=dma(kvh), rh=dma(kvh),
     )
     names = [*ins, "out", *scratch]

time: 62.4 us -> 62.1 us (level)
  no operation moved by 1% of the time
where the time goes in v3:
time: 62.1 us; the launch traced here: 61.9 us
  Pallas kernels  60.4 us (97%)
  local copies, waits for them, and re-layouts  1.47 us (2%)
    pallas_call x1, Pallas kernels, body(): pl.pallas_call(run, name='fused', out_shape=jax.ShapeDtypeStruct((qtok, c...  60.4 us
    unnamed x1, local copies, waits for them, and re-layouts  1.47 us

profile of v3, /device:TPU:0, one launch (start us, length us, event | category | flops | bytes accessed | tf_op | source)
XLA Modules:
  0.0 61.9 jit_solution(136264706090590416)
XLA Ops:
  0.0 60.4 %fused.1 = bf16[32,1024]{1,0:T(8,128)(2,1)} custom-call(s32[32]{0:T(128)} %refs_0_.1, s32[16]{0:T(128)} %refs_1_.1, s32[32]{0:T(128)} %refs_2_.1, f32[4,16]{1,0:T(4,128)} %bitcast.2, f32[4,16]{1,0:T(4,128)} %bitcast.3, bf16[32,1024]{1,0:T(8,128)(2,1)} %refs_5_.1, bf16[1024,8192]{1,0:T(8,128)(2,1)} %refs_6_.1, bf16[1024,512]{1,0:T(8,128)(2,1)} %refs_7_.1, ...), custom_call_target="tpu_custom_call" | custom-call | tf_op jit(solution)/shard_map/fused/pallas_call | solution.py:618
  60.5 1.5 %copy.16 = bf16[32,1024]{1,0:T(8,128)(2,1)} copy(bf16[32,1024]{1,0:T(8,128)(2,1)} %fused.1) | data formatting | bytes 131072

commit v4 on v3

--- a/solution.py
+++ b/solution.py
@@ -207,11 +207,50 @@
         loop(chips - 1, lambda k: landing(buf, send, recv, k + 1).wait_recv())
         forward(buf, fsend, frecv).start()
 
+    def g_spread(g, i):
+        piece = g.buf.at[core, near, far]
+        return remote(piece, piece, g.sz.at[i], g.rz.at[i], device(up(i), near, core))
+
+    def g_land(g, i):
+        piece = g.buf.at[core, near, down(i)]
+        return remote(piece, piece, g.sz.at[i], g.rz.at[i], device(up(i), near, core))
+
+    def crossing(g, n):
+        return remote(g.buf.at[core, n], g.buf.at[core, n], g.sy, g.ry, across)
+
+    def passing(g, c):
+        return remote(g.buf.at[c], g.buf.at[c], g.sp, g.rp, partner)
+
+    def gather_far(g):
+        loop(half - 1, lambda i: g_spread(g, i + 1).start())
+
+    def gather_side(g):
+        loop(half - 1, lambda i: g_land(g, i + 1).wait_recv())
+        crossing(g, near).start()
+
+    def gather_pair(g):
+        crossing(g, 1 - near).wait_recv()
+        passing(g, core).start()
+
+    def gather_end(g):
+        passing(g, 1 - core).wait_recv()
+
+    def gather_sent(g):
+        loop(half - 1, lambda i: g_spread(g, i + 1).wait_send())
+        crossing(g, near).wait_send()
+        passing(g, core).wait_send()
+
+    def gather(buf, sems, h):
+        sz, rz, sy, ry, sp, rp = sems
+        return types.SimpleNamespace(
+            buf=buf, sz=sz.at[h], rz=rz.at[h], sy=sy.at[h], ry=ry.at[h], sp=sp.at[h], rp=rp.at[h]
+        )
+
     def q_gather(h):
-        return r.gat.at[h], r.sg.at[h], r.rg.at[h]
+        return gather(r.gat.at[h], (r.qsz, r.qrz, r.qsy, r.qry, r.qsp, r.qrp), h)
 
     def kv_gather():
-        return r.gkv, r.ksg, r.krg
+        return gather(r.gkv, (r.kgsz, r.kgrz, r.kgsy, r.kgry, r.kgsp, r.kgrp), 0)
 
     def o_gather(h):
         return r.agat.at[h], r.sa.at[h], r.ra.at[h]
@@ -244,7 +283,7 @@
             long(h, i).wait_recv()
             total = total + r.zrecv[h, i - 1]
         r.gat[h, core, near, far] = total.astype(BF16)
-        spread_out(*q_gather(h))
+        gather_far(q_gather(h))
 
     def stage_d_kv():
         total = r.kz[pl.ds(far * cfg.kuz, cfg.kuz)]
@@ -252,10 +291,7 @@
             long_kv(i).wait_recv()
             total = total + r.kzrecv[i - 1]
         r.gkv[core, near, far] = total.astype(BF16)
-        spread_out(*kv_gather())
-
-    def stage_e(h):
-        pass_on(*q_gather(h), r.sf.at[h], r.rf.at[h])
+        gather_far(kv_gather())
 
     def front(i):
         @pl.when(i < kvh)
@@ -300,9 +336,12 @@
     project_kv()
     pair_kv().start()
     loop(kvh + 4, lambda i: front(i + 1))
-    stage_e(0)
-    pass_on(*kv_gather(), r.ksf.at[0], r.krf.at[0])
-    arrived(r.gkv, r.ksf.at[0], r.krf.at[0]).wait_recv()
+    gather_side(q_gather(0))
+    gather_side(kv_gather())
+    gather_side(q_gather(1))
+    gather_pair(q_gather(0))
+    gather_pair(kv_gather())
+    gather_end(kv_gather())
 
     first_row = lax.broadcasted_iota(jnp.int32, (STAT, rows), 0) == 0
     deep = tz * group
@@ -410,52 +449,62 @@
             own = nt(q, self_k) * const + jnp.concatenate(bias, axis=0)
             return jnp.concatenate(demo, axis=0), own
 
-        def first(b):
+        def first():
             return jnp.full((rows, blk), NEG, F32)
 
-        q = query(0)
-        run = first(0)
-        for j in range(steps):
-            run = score(0, j, q, run)
-        for b in range(blocks):
-            s_demo, s_self = small_scores(b, q)
-            top = jnp.maximum(
-                jnp.max(run, axis=1, keepdims=True),
-                jnp.maximum(
-                    jnp.max(s_demo, axis=1, keepdims=True), jnp.max(s_self, axis=1, keepdims=True)
-                ),
-            )
-            e_demo, e_self = jnp.exp2(s_demo - top), jnp.exp2(s_self - top)
-            total = jnp.sum(e_demo, axis=1, keepdims=True) + jnp.sum(e_self, axis=1, keepdims=True)
-            w_demo, w_self = e_demo.astype(BF16), e_self.astype(BF16)
-            sums = jnp.zeros((rows, blk), F32)
-            if b + 1 < blocks:
-                q = query(b + 1)
-                run = first(b + 1)
-            for j in range(steps):
-                for e in range(2):
-                    at = 2 * j + e
-                    lanes = slice(at * blk, (at + 1) * blk)
-                    x = jnp.exp2(r.scr[b % 2][:, lanes] - top)
-                    sums = sums + x
-                    r.wts[b % 2][:, lanes] = (x * r.vs[h, at]).astype(BF16)
-                if b + 1 < blocks:
-                    run = score(b + 1, j, q, run)
-            total = total + jnp.sum(sums, axis=1, keepdims=True)
-            value = nn(r.wts[b % 2][...], r.pvb[h]) + nn(w_self, self_v)
+        def finish(b, e):
+            total = e.total + jnp.sum(e.sums, axis=1, keepdims=True)
+            value = nn(r.wts[b % 2][...], r.pvb[h]) + nn(e.w_self, self_v)
             value = value + jnp.concatenate(
                 [
-                    nn(w_demo[t * group : (t + 1) * group], r.dvb[h, r.tasks[b * tq + t]])
+                    nn(e.w_demo[t * group : (t + 1) * group], r.dvb[h, r.tasks[b * tq + t]])
                     for t in range(tq)
                 ],
                 axis=0,
             )
             lane = lax.broadcasted_iota(jnp.int32, (rows, HD), 1)
             c, n = b // SIDES, b % SIDES
-            r.pstat[h, c, n] = jnp.where(lane == 0, top, total).T[:STAT]
+            r.pstat[h, c, n] = jnp.where(lane == 0, e.top, total).T[:STAT]
             r.pval[h, c, n] = value
+
+        q = query(0)
+        run = first()
+        for j in range(steps):
+            run = score(0, j, q, run)
+        s_demo, s_self = small_scores(0, q)
+        before = None
+        for b in range(blocks):
+            e = types.SimpleNamespace()
+            e.top = jnp.maximum(
+                jnp.max(run, axis=1, keepdims=True),
+                jnp.maximum(
+                    jnp.max(s_demo, axis=1, keepdims=True), jnp.max(s_self, axis=1, keepdims=True)
+                ),
+            )
+            e_demo, e_self = jnp.exp2(s_demo - e.top), jnp.exp2(s_self - e.top)
+            e.total = jnp.sum(e_demo, axis=1, keepdims=True)
+            e.total = e.total + jnp.sum(e_self, axis=1, keepdims=True)
+            e.w_demo, e.w_self = e_demo.astype(BF16), e_self.astype(BF16)
+            e.sums = jnp.zeros((rows, blk), F32)
+            if b + 1 < blocks:
+                q = query(b + 1)
+                run = first()
+            for j in range(steps):
+                for p in range(2):
+                    at = 2 * j + p
+                    lanes = slice(at * blk, (at + 1) * blk)
+                    x = jnp.exp2(r.scr[b % 2][:, lanes] - e.top)
+                    e.sums = e.sums + x
+                    r.wts[b % 2][:, lanes] = (x * r.vs[h, at]).astype(BF16)
+                if b + 1 < blocks:
+                    run = score(b + 1, j, q, run)
+                if j == 0 and before is not None:
+                    finish(b - 1, before)
+            if b + 1 < blocks:
+                s_demo, s_self = small_scores(b + 1, q)
+            before = e
             between(b)
-
+        finish(blocks - 1, before)
         start(send_pair(h))
 
     def relay(h):
@@ -470,23 +519,25 @@
         )
         r.acc[...] += nn(left, r.wob[h])
 
+    chores = (
+        (0, 0, lambda: gather_side(q_gather(2))),
+        (0, 1, lambda: gather_pair(q_gather(1))),
+        (0, 2, lambda: gather_side(q_gather(3))),
+        (1, 0, lambda: merge_pair(0)),
+        (1, 1, lambda: gather_pair(q_gather(2))),
+        (2, 0, lambda: merge_pair(1)),
+        (2, 1, lambda: gather_pair(q_gather(3))),
+        (3, 0, lambda: merge_pair(2)),
+        (3, 2, lambda: merge_own(0)),
+    )
+
     def middle(h):
-        arrived(r.gat.at[h], r.sf.at[h], r.rf.at[h]).wait_recv()
+        gather_end(q_gather(h))
+
         def between(b):
-            if b == 0:
-                @pl.when(h > 0)
-                def _():
-                    merge_pair(h - 1)
-
-            if b == 1:
-                @pl.when(h + 1 < kvh)
-                def _():
-                    stage_e(h + 1)
-
-            if b == 2:
-                @pl.when(h == kvh - 1)
-                def _():
-                    merge_own(0)
+            for at, block, chore in chores:
+                if block == b:
+                    pl.when(h == at)(chore)
 
         attend(h, between)
 
@@ -522,9 +573,9 @@
         pair(h).wait_send()
         cross(h).wait_send()
         loop(half - 1, lambda i: long(h, i + 1).wait_send())
-        for buf, send, recv in (q_gather(h), o_gather(h)):
-            loop(chips - 1, lambda k: spreading(buf, send, recv, k + 1).wait_send())
-        forward(r.gat.at[h], r.sf.at[h], r.rf.at[h]).wait_send()
+        gather_sent(q_gather(h))
+        buf, send, recv = o_gather(h)
+        loop(chips - 1, lambda k: spreading(buf, send, recv, k + 1).wait_send())
         forward(r.agat.at[h], r.sh.at[h], r.rh.at[h]).wait_send()
         sent(send_pair(h))
         loop(chips - 1, lambda k: sent(send_own(h, k + 1)))
@@ -533,9 +584,7 @@
     pair_kv().wait_send()
     cross_kv().wait_send()
     loop(half - 1, lambda i: long_kv(i + 1).wait_send())
-    buf, send, recv = kv_gather()
-    loop(chips - 1, lambda k: spreading(buf, send, recv, k + 1).wait_send())
-    forward(r.gkv, r.ksf.at[0], r.krf.at[0]).wait_send()
+    gather_sent(kv_gather())
 
 
 def body(
@@ -599,10 +648,14 @@
         s_in=dma(3), s_wq=dma(kvh * nch), s_wo=dma(kvh),
         c_pk=dma(kvh), c_pv=dma(kvh), c_dk=dma(kvh), c_dv=dma(kvh),
         s1=dma(kvh), r1=dma(kvh), sy=dma(kvh), ry=dma(kvh),
-        sz=dma(kvh, half - 1), rz=dma(kvh, half - 1), sg=dma(kvh, chips), rg=dma(kvh, chips),
-        sf=dma(kvh), rf=dma(kvh),
+        sz=dma(kvh, half - 1), rz=dma(kvh, half - 1),
         ks1=dma(1), kr1=dma(1), ksy=dma(1), kry=dma(1), ksz=dma(half - 1), krz=dma(half - 1),
-        ksg=dma(chips), krg=dma(chips), ksf=dma(1), krf=dma(1),
+        **{
+            f"{g}{d}{e}": dma(n, half) if e == "z" else dma(n)
+            for g, n in (("q", kvh), ("kg", 1))
+            for d in "sr"
+            for e in "zyp"
+        },
         **{f"{d}_{e}": dma(kvh) for d in "sr" for e in ("pv", "ps")},
         **{f"{d}_{e}": dma(kvh, chips) for d in "sr" for e in ("ov", "os")},
         sa=dma(kvh, chips), ra=dma(kvh, chips), sh=dma(kvh), rh=dma(kvh),

time: 62.1 us -> 59.4 us (0.957)
  Pallas kernels: 60.4 us -> 57.7 us
    pallas_call x1, Pallas kernels: 60.4 us -> 57.7 us  [body(): pl.pallas_call(run, name='fused', out_shape=jax.ShapeDtypeStruct((qtok, c...]
where the time goes in v4:
time: 59.4 us; the launch traced here: 59.2 us
  Pallas kernels  57.7 us (97%)
  local copies, waits for them, and re-layouts  1.47 us (2%)
    pallas_call x1, Pallas kernels, body(): pl.pallas_call(run, name='fused', out_shape=jax.ShapeDtypeStruct((qtok, c...  57.7 us
    unnamed x1, local copies, waits for them, and re-layouts  1.47 us

profile of v4, /device:TPU:0, one launch (start us, length us, event | category | flops | bytes accessed | tf_op | source)
XLA Modules:
  0.0 59.2 jit_solution(15420761426700271721)
XLA Ops:
  0.0 57.7 %fused.1 = bf16[32,1024]{1,0:T(8,128)(2,1)} custom-call(s32[32]{0:T(128)} %refs_0_.1, s32[16]{0:T(128)} %refs_1_.1, s32[32]{0:T(128)} %refs_2_.1, f32[4,16]{1,0:T(4,128)} %bitcast.2, f32[4,16]{1,0:T(4,128)} %bitcast.3, bf16[32,1024]{1,0:T(8,128)(2,1)} %refs_5_.1, bf16[1024,8192]{1,0:T(8,128)(2,1)} %refs_6_.1, bf16[1024,512]{1,0:T(8,128)(2,1)} %refs_7_.1, ...), custom_call_target="tpu_custom_call" | custom-call | tf_op jit(solution)/shard_map/fused/pallas_call | solution.py:671
  57.8 1.5 %copy.16 = bf16[32,1024]{1,0:T(8,128)(2,1)} copy(bf16[32,1024]{1,0:T(8,128)(2,1)} %fused.1) | data formatting | bytes 131072

commit v5 on v4

--- a/solution.py
+++ b/solution.py
@@ -78,10 +78,10 @@
     def load_cache(h):
         lanes = pl.ds(pl.multiple_of(h * HD, HD), HD)
         return (
-            pltpu.make_async_copy(r.pk.at[:, lanes], r.pkb.at[h], r.c_pk.at[h]),
-            pltpu.make_async_copy(r.dk.at[:, :, lanes], r.dkb.at[h], r.c_dk.at[h]),
-            pltpu.make_async_copy(r.pv.at[:, lanes], r.pvb.at[h], r.c_pv.at[h]),
-            pltpu.make_async_copy(r.dv.at[:, :, lanes], r.dvb.at[h], r.c_dv.at[h]),
+            pltpu.make_async_copy(r.pk.at[:, lanes], r.pkb.at[h], r.c_pk.at[0]),
+            pltpu.make_async_copy(r.dk.at[:, :, lanes], r.dkb.at[h], r.c_dk.at[0]),
+            pltpu.make_async_copy(r.pv.at[:, lanes], r.pvb.at[h], r.c_pv.at[0]),
+            pltpu.make_async_copy(r.dv.at[:, :, lanes], r.dvb.at[h], r.c_dv.at[0]),
         )
 
     small = [
@@ -177,22 +177,31 @@
     def long(h, i):
         return remote(
             r.zbuf.at[h, pl.ds(up(i) * tz, tz)], r.zrecv.at[h, i - 1],
-            r.sz.at[h, i - 1], r.rz.at[h, i - 1], device(up(i), near, core),
-        )
+            r.sz.at[h], r.rz.at[h], device(up(i), near, core),
+        )
+
+    def long_all(h):
+        return remote(r.zrecv.at[h], r.zrecv.at[h], r.sz.at[h], r.rz.at[h], partner)
+
+    def long_kv_all():
+        return remote(r.kzrecv, r.kzrecv, r.ksz.at[0], r.krz.at[0], partner)
 
     def long_kv(i):
         return remote(
             r.kz.at[pl.ds(up(i) * cfg.kuz, cfg.kuz)], r.kzrecv.at[i - 1],
-            r.ksz.at[i - 1], r.krz.at[i - 1], device(up(i), near, core),
+            r.ksz.at[0], r.krz.at[0], device(up(i), near, core),
         )
 
     def spreading(buf, send, recv, k):
         piece = buf.at[core, near, far]
-        return remote(piece, piece, send.at[k], recv.at[k], chip_at(k))
-
-    def landing(buf, send, recv, k):
-        piece = buf.at[core, side(k), down(k // 2)]
-        return remote(piece, piece, send.at[k], recv.at[k], chip_at(k))
+        return remote(piece, piece, send, recv, chip_at(k))
+
+    def spread_out(buf, send, recv):
+        loop(chips - 1, lambda k: spreading(buf, send, recv, k + 1).start())
+
+    def spread_all(send, recv):
+        pieces = r.ogot.at[0, pl.ds(1, chips - 1)]
+        return remote(pieces, pieces, send, recv, partner)
 
     def forward(buf, send, recv):
         return remote(buf.at[core], buf.at[core], send, recv, partner)
@@ -200,20 +209,17 @@
     def arrived(buf, send, recv):
         return remote(buf.at[1 - core], buf.at[1 - core], send, recv, partner)
 
-    def spread_out(buf, send, recv):
-        loop(chips - 1, lambda k: spreading(buf, send, recv, k + 1).start())
-
     def pass_on(buf, send, recv, fsend, frecv):
-        loop(chips - 1, lambda k: landing(buf, send, recv, k + 1).wait_recv())
+        spread_all(send, recv).wait_recv()
         forward(buf, fsend, frecv).start()
 
     def g_spread(g, i):
         piece = g.buf.at[core, near, far]
-        return remote(piece, piece, g.sz.at[i], g.rz.at[i], device(up(i), near, core))
-
-    def g_land(g, i):
-        piece = g.buf.at[core, near, down(i)]
-        return remote(piece, piece, g.sz.at[i], g.rz.at[i], device(up(i), near, core))
+        return remote(piece, piece, g.sz, g.rz, device(up(i), near, core))
+
+    def g_all(g):
+        pieces = g.buf.at[core, near, pl.ds(0, half - 1)]
+        return remote(pieces, pieces, g.sz, g.rz, partner)
 
     def crossing(g, n):
         return remote(g.buf.at[core, n], g.buf.at[core, n], g.sy, g.ry, across)
@@ -225,7 +231,7 @@
         loop(half - 1, lambda i: g_spread(g, i + 1).start())
 
     def gather_side(g):
-        loop(half - 1, lambda i: g_land(g, i + 1).wait_recv())
+        g_all(g).wait_recv()
         crossing(g, near).start()
 
     def gather_pair(g):
@@ -236,7 +242,7 @@
         passing(g, 1 - core).wait_recv()
 
     def gather_sent(g):
-        loop(half - 1, lambda i: g_spread(g, i + 1).wait_send())
+        g_all(g).wait_send()
         crossing(g, near).wait_send()
         passing(g, core).wait_send()
 
@@ -279,16 +285,23 @@
 
     def stage_d(h):
         total = r.zbuf[h, pl.ds(far * tz, tz)]
+        long_all(h).wait_recv()
         for i in range(1, half):
-            long(h, i).wait_recv()
             total = total + r.zrecv[h, i - 1]
         r.gat[h, core, near, far] = total.astype(BF16)
-        gather_far(q_gather(h))
+
+        @pl.when(h < kvh - 1)
+        def _():
+            gather_far(q_gather(h))
+
+        @pl.when(h == kvh - 1)
+        def _():
+            spread_out(r.gat.at[h], r.sg.at[0], r.rg.at[0])
 
     def stage_d_kv():
         total = r.kz[pl.ds(far * cfg.kuz, cfg.kuz)]
+        long_kv_all().wait_recv()
         for i in range(1, half):
-            long_kv(i).wait_recv()
             total = total + r.kzrecv[i - 1]
         r.gkv[core, near, far] = total.astype(BF16)
         gather_far(kv_gather())
@@ -360,11 +373,22 @@
         return (
             remote(
                 r.oval.at[h, side(k), up(k // 2)], r.ogot.at[h, k],
-                r.s_ov.at[h, k], r.r_ov.at[h, k], chip_at(k),
+                r.s_ov.at[h], r.r_ov.at[h], chip_at(k),
             ),
             remote(
                 r.ostat.at[h, side(k)], r.ogots.at[h, k],
-                r.s_os.at[h, k], r.r_os.at[h, k], chip_at(k),
+                r.s_os.at[h], r.r_os.at[h], chip_at(k),
+            ),
+        )
+
+    def send_own_all(h):
+        every = pl.ds(1, chips - 1)
+        return (
+            remote(
+                r.ogot.at[h, every], r.ogot.at[h, every], r.s_ov.at[h], r.r_ov.at[h], partner
+            ),
+            remote(
+                r.ogots.at[h, every], r.ogots.at[h, every], r.s_os.at[h], r.r_os.at[h], partner
             ),
         )
 
@@ -394,7 +418,7 @@
         loop(chips - 1, lambda k: start(send_own(h, k + 1)))
 
     def merge_own(h):
-        loop(chips - 1, lambda k: receive(send_own(h, k + 1)))
+        receive(send_own_all(h))
         stats = [r.ostat[h, near], *[r.ogots[h, k] for k in range(1, chips)]]
         top = functools.reduce(jnp.maximum, [s[:1] for s in stats])
         factors = [jnp.exp2(s[:1] - top) for s in stats]
@@ -519,14 +543,18 @@
         )
         r.acc[...] += nn(left, r.wob[h])
 
+    last = kvh - 1
+
+    def last_query():
+        pass_on(r.gat.at[last], r.sg.at[0], r.rg.at[0], r.qsp.at[last], r.qrp.at[last])
+
     chores = (
         (0, 0, lambda: gather_side(q_gather(2))),
         (0, 1, lambda: gather_pair(q_gather(1))),
-        (0, 2, lambda: gather_side(q_gather(3))),
         (1, 0, lambda: merge_pair(0)),
         (1, 1, lambda: gather_pair(q_gather(2))),
         (2, 0, lambda: merge_pair(1)),
-        (2, 1, lambda: gather_pair(q_gather(3))),
+        (1, 2, last_query),
         (3, 0, lambda: merge_pair(2)),
         (3, 2, lambda: merge_own(0)),
     )
@@ -541,11 +569,11 @@
 
         attend(h, between)
 
-    def cached(h):
-        for copy in load_cache(h):
-            copy.wait()
-
-    loop(kvh, cached)
+    for buf, sem in (
+        (r.pkb, r.c_pk), (r.dkb, r.c_dk), (r.pvb, r.c_pv), (r.dvb, r.c_dv),
+    ):
+        pltpu.make_async_copy(buf, buf, sem.at[0]).wait()
+
     loop(kvh, middle)
     merge_pair(kvh - 1)
 
@@ -572,18 +600,25 @@
     def drain(h):
         pair(h).wait_send()
         cross(h).wait_send()
-        loop(half - 1, lambda i: long(h, i + 1).wait_send())
-        gather_sent(q_gather(h))
+        long_all(h).wait_send()
+        passing(q_gather(h), core).wait_send()
+
+        @pl.when(h < kvh - 1)
+        def _():
+            g_all(q_gather(h)).wait_send()
+            crossing(q_gather(h), near).wait_send()
+
         buf, send, recv = o_gather(h)
-        loop(chips - 1, lambda k: spreading(buf, send, recv, k + 1).wait_send())
+        spread_all(send, recv).wait_send()
         forward(r.agat.at[h], r.sh.at[h], r.rh.at[h]).wait_send()
         sent(send_pair(h))
-        loop(chips - 1, lambda k: sent(send_own(h, k + 1)))
+        sent(send_own_all(h))
 
     loop(kvh, drain)
+    spread_all(r.sg.at[0], r.rg.at[0]).wait_send()
     pair_kv().wait_send()
     cross_kv().wait_send()
-    loop(half - 1, lambda i: long_kv(i + 1).wait_send())
+    long_kv_all().wait_send()
     gather_sent(kv_gather())
 
 
@@ -646,19 +681,19 @@
         agat=v((kvh, 2, SIDES, half, tz, group, HD), BF16),
         flat=v((qtok * group, HD), F32), acc=v((qtok, cols), F32),
         s_in=dma(3), s_wq=dma(kvh * nch), s_wo=dma(kvh),
-        c_pk=dma(kvh), c_pv=dma(kvh), c_dk=dma(kvh), c_dv=dma(kvh),
+        c_pk=dma(1), c_pv=dma(1), c_dk=dma(1), c_dv=dma(1),
         s1=dma(kvh), r1=dma(kvh), sy=dma(kvh), ry=dma(kvh),
-        sz=dma(kvh, half - 1), rz=dma(kvh, half - 1),
-        ks1=dma(1), kr1=dma(1), ksy=dma(1), kry=dma(1), ksz=dma(half - 1), krz=dma(half - 1),
+        sz=dma(kvh), rz=dma(kvh),
+        ks1=dma(1), kr1=dma(1), ksy=dma(1), kry=dma(1), ksz=dma(1), krz=dma(1),
         **{
-            f"{g}{d}{e}": dma(n, half) if e == "z" else dma(n)
+            f"{g}{d}{e}": dma(n)
             for g, n in (("q", kvh), ("kg", 1))
             for d in "sr"
             for e in "zyp"
         },
         **{f"{d}_{e}": dma(kvh) for d in "sr" for e in ("pv", "ps")},
-        **{f"{d}_{e}": dma(kvh, chips) for d in "sr" for e in ("ov", "os")},
-        sa=dma(kvh, chips), ra=dma(kvh, chips), sh=dma(kvh), rh=dma(kvh),
+        **{f"{d}_{e}": dma(kvh) for d in "sr" for e in ("ov", "os")},
+        sa=dma(kvh), ra=dma(kvh), sg=dma(1), rg=dma(1), sh=dma(kvh), rh=dma(kvh),
     )
     names = [*ins, "out", *scratch]
 

time: 59.4 us -> 56.7 us (0.955)
  Pallas kernels: 57.7 us -> 55.1 us
    pallas_call x1, Pallas kernels: 57.7 us -> 55.1 us  [body(): pl.pallas_call(run, name='fused', out_shape=jax.ShapeDtypeStruct((qtok, c...]
where the time goes in v5:
time: 56.7 us; the launch traced here: 56.5 us
  Pallas kernels  55.1 us (97%)
  local copies, waits for them, and re-layouts  1.47 us (3%)
    pallas_call x1, Pallas kernels, body(): pl.pallas_call(run, name='fused', out_shape=jax.ShapeDtypeStruct((qtok, c...  55.1 us
    unnamed x1, local copies, waits for them, and re-layouts  1.47 us

profile of v5, /device:TPU:0, one launch (start us, length us, event | category | flops | bytes accessed | tf_op | source)
XLA Modules:
  0.0 56.5 jit_solution(7517156239187926998)
XLA Ops:
  0.0 55.1 %fused.1 = bf16[32,1024]{1,0:T(8,128)(2,1)} custom-call(s32[32]{0:T(128)} %refs_0_.1, s32[16]{0:T(128)} %refs_1_.1, s32[32]{0:T(128)} %refs_2_.1, f32[4,16]{1,0:T(4,128)} %bitcast.2, f32[4,16]{1,0:T(4,128)} %bitcast.3, bf16[32,1024]{1,0:T(8,128)(2,1)} %refs_5_.1, bf16[1024,8192]{1,0:T(8,128)(2,1)} %refs_6_.1, bf16[1024,512]{1,0:T(8,128)(2,1)} %refs_7_.1, ...), custom_call_target="tpu_custom_call" | custom-call | tf_op jit(solution)/shard_map/fused/pallas_call | solution.py:706
  55.1 1.5 %copy.16 = bf16[32,1024]{1,0:T(8,128)(2,1)} copy(bf16[32,1024]{1,0:T(8,128)(2,1)} %fused.1) | data formatting | bytes 131072

commit v6 on v5

--- a/solution.py
+++ b/solution.py
@@ -88,7 +88,18 @@
         pltpu.make_async_copy(src, dst, r.s_in.at[i])
         for i, (src, dst) in enumerate(((r.hid, r.hidb), (r.wk, r.wkb), (r.wv, r.wvb)))
     ]
+    scalars = [
+        pltpu.make_async_copy(src, dst, r.s_sc.at[i])
+        for i, (src, dst) in enumerate(
+            (
+                (r.tasks_in, r.tasks), (r.lens_in, r.lens), (r.offs_in, r.offs),
+                (r.ks_in, r.ks), (r.vs_in, r.vs),
+            )
+        )
+    ]
     small[0].start()
+    for copy in scalars:
+        copy.start()
     loop(nch, lambda k: load_wq(k).start())
     small[1].start()
     small[2].start()
@@ -115,6 +126,8 @@
 
     loop(chips - 1, lambda k: hello(chip_at(k + 1)))
 
+    for copy in scalars:
+        copy.wait()
     lane_d = lax.broadcasted_iota(jnp.int32, (1, cfg.demo_dev), 1)
     lane_t = lax.broadcasted_iota(jnp.int32, (1, qtok), 1)
 
@@ -283,6 +296,11 @@
         r.kz[...] = r.kown[...] + r.kyrecv[...]
         loop(half - 1, lambda i: long_kv(i + 1).start())
 
+    direct = (kvh - 1,)
+
+    def is_direct(h):
+        return functools.reduce(jnp.logical_or, [h == d for d in direct], h < 0)
+
     def stage_d(h):
         total = r.zbuf[h, pl.ds(far * tz, tz)]
         long_all(h).wait_recv()
@@ -290,13 +308,13 @@
             total = total + r.zrecv[h, i - 1]
         r.gat[h, core, near, far] = total.astype(BF16)
 
-        @pl.when(h < kvh - 1)
+        @pl.when(is_direct(h))
+        def _():
+            spread_out(r.gat.at[h], r.qsz.at[h], r.qrz.at[h])
+
+        @pl.when(jnp.logical_not(is_direct(h)))
         def _():
             gather_far(q_gather(h))
-
-        @pl.when(h == kvh - 1)
-        def _():
-            spread_out(r.gat.at[h], r.sg.at[0], r.rg.at[0])
 
     def stage_d_kv():
         total = r.kz[pl.ds(far * cfg.kuz, cfg.kuz)]
@@ -306,6 +324,16 @@
         r.gkv[core, near, far] = total.astype(BF16)
         gather_far(kv_gather())
 
+    def query_far(h):
+        if h not in direct:
+            gather_side(q_gather(h))
+
+    def query_near(h):
+        if h in direct:
+            pass_on(r.gat.at[h], r.qsz.at[h], r.qrz.at[h], r.qsp.at[h], r.qrp.at[h])
+        else:
+            gather_pair(q_gather(h))
+
     def front(i):
         @pl.when(i < kvh)
         def _():
@@ -335,6 +363,11 @@
             loop(kvh, caches)
             loop(kvh, lambda h: load_wo(h).start())
 
+        @pl.when(i == 8)
+        def _():
+            query_far(0)
+            gather_side(kv_gather())
+
         @pl.when(i >= 5)
         def _():
             stage_d(i - 5)
@@ -342,6 +375,10 @@
         @pl.when(i == 5)
         def _():
             stage_d_kv()
+
+        @pl.when(i == 8)
+        def _():
+            query_far(1)
 
     project(0)
     pl.semaphore_wait(barrier, chips)
@@ -349,13 +386,6 @@
     project_kv()
     pair_kv().start()
     loop(kvh + 4, lambda i: front(i + 1))
-    gather_side(q_gather(0))
-    gather_side(kv_gather())
-    gather_side(q_gather(1))
-    gather_pair(q_gather(0))
-    gather_pair(kv_gather())
-    gather_end(kv_gather())
-
     first_row = lax.broadcasted_iota(jnp.int32, (STAT, rows), 0) == 0
     deep = tz * group
 
@@ -543,18 +573,14 @@
         )
         r.acc[...] += nn(left, r.wob[h])
 
-    last = kvh - 1
-
-    def last_query():
-        pass_on(r.gat.at[last], r.sg.at[0], r.rg.at[0], r.qsp.at[last], r.qrp.at[last])
-
     chores = (
-        (0, 0, lambda: gather_side(q_gather(2))),
-        (0, 1, lambda: gather_pair(q_gather(1))),
+        (0, 0, lambda: query_far(2)),
+        (0, 1, lambda: query_near(1)),
+        (0, 2, lambda: query_far(3)),
         (1, 0, lambda: merge_pair(0)),
-        (1, 1, lambda: gather_pair(q_gather(2))),
+        (1, 1, lambda: query_near(2)),
         (2, 0, lambda: merge_pair(1)),
-        (1, 2, last_query),
+        (1, 2, lambda: query_near(3)),
         (3, 0, lambda: merge_pair(2)),
         (3, 2, lambda: merge_own(0)),
     )
@@ -574,6 +600,9 @@
     ):
         pltpu.make_async_copy(buf, buf, sem.at[0]).wait()
 
+    query_near(0)
+    gather_pair(kv_gather())
+    gather_end(kv_gather())
     loop(kvh, middle)
     merge_pair(kvh - 1)
 
@@ -603,7 +632,11 @@
         long_all(h).wait_send()
         passing(q_gather(h), core).wait_send()
 
-        @pl.when(h < kvh - 1)
+        @pl.when(is_direct(h))
+        def _():
+            spread_all(r.qsz.at[h], r.qrz.at[h]).wait_send()
+
+        @pl.when(jnp.logical_not(is_direct(h)))
         def _():
             g_all(q_gather(h)).wait_send()
             crossing(q_gather(h), near).wait_send()
@@ -615,7 +648,6 @@
         sent(send_own_all(h))
 
     loop(kvh, drain)
-    spread_all(r.sg.at[0], r.rg.at[0]).wait_send()
     pair_kv().wait_send()
     cross_kv().wait_send()
     long_kv_all().wait_send()
@@ -647,16 +679,20 @@
         blk=pre_dev // key_scales.shape[0], rows=rows, nch=nch, cw=cw, demo_dev=demo_dev,
         pre_dev=pre_dev, kuz=kuz,
     )
-    smem = pl.BlockSpec(memory_space=pltpu.SMEM)
     hbm = pl.BlockSpec(memory_space=pltpu.HBM)
-    ins = ["tasks", "lens", "offs", "ks", "vs"]
+    ins = ["tasks_in", "lens_in", "offs_in", "ks_in", "vs_in"]
     ins += ["hid", "wq", "wk", "wv", "wo", "pk", "pv", "dk", "dv"]
     v = pltpu.VMEM
 
     def dma(*shape):
         return pltpu.SemaphoreType.DMA(shape)
 
+    nblk = key_scales.shape[0]
+    smem = pltpu.SMEM
     scratch = dict(
+        tasks=smem((qtok,), jnp.int32), lens=smem((tasks,), jnp.int32),
+        offs=smem((qtok,), jnp.int32), ks=smem((kvh, nblk), F32), vs=smem((kvh, nblk), F32),
+        s_sc=dma(5),
         hidb=v(hidden.shape, BF16), wkb=v(w_key.shape, BF16), wvb=v(w_value.shape, BF16),
         wqb=v((kvh * nch, depth, cw), BF16), wob=v((kvh, group * HD, cols), BF16),
         pkb=v((kvh, pre_dev, HD), BF16), pvb=v((kvh, pre_dev, HD), BF16),
@@ -693,7 +729,7 @@
         },
         **{f"{d}_{e}": dma(kvh) for d in "sr" for e in ("pv", "ps")},
         **{f"{d}_{e}": dma(kvh) for d in "sr" for e in ("ov", "os")},
-        sa=dma(kvh), ra=dma(kvh), sg=dma(1), rg=dma(1), sh=dma(kvh), rh=dma(kvh),
+        sa=dma(kvh), ra=dma(kvh), sh=dma(kvh), rh=dma(kvh),
     )
     names = [*ins, "out", *scratch]
 
@@ -707,7 +743,7 @@
         run,
         name="fused",
         out_shape=jax.ShapeDtypeStruct((qtok, cols), BF16),
-        in_specs=[smem] * 5 + [hbm] * 9,
+        in_specs=[hbm] * 14,
         out_specs=pl.BlockSpec(memory_space=pltpu.VMEM),
         scratch_shapes=list(scratch.values()),
         compiler_params=pltpu.CompilerParams(

time: 56.7 us -> 54.9 us (0.968)
  Pallas kernels: 55.1 us -> 53.2 us
    pallas_call x1, Pallas kernels: 55.1 us -> 53.2 us  [body(): pl.pallas_call(run, name='fused', out_shape=jax.ShapeDtypeStruct((qtok, c...]
where the time goes in v6:
time: 54.9 us; the launch traced here: 54.7 us
  Pallas kernels  53.2 us (97%)
  local copies, waits for them, and re-layouts  1.47 us (3%)
    pallas_call x1, Pallas kernels, body(): pl.pallas_call(run, name='fused', out_shape=jax.ShapeDtypeStruct((qtok, c...  53.2 us
    unnamed x1, local copies, waits for them, and re-layouts  1.47 us

profile of v6, /device:TPU:0, one launch (start us, length us, event | category | flops | bytes accessed | tf_op | source)
XLA Modules:
  0.0 54.7 jit_solution(8475677920254391303)
XLA Ops:
  0.0 53.2 %fused.1 = bf16[32,1024]{1,0:T(8,128)(2,1)} custom-call(s32[32]{0:T(128)} %refs_0_.1, s32[16]{0:T(128)} %refs_1_.1, s32[32]{0:T(128)} %refs_2_.1, f32[4,16]{1,0:T(4,128)} %bitcast.2, f32[4,16]{1,0:T(4,128)} %bitcast.3, bf16[32,1024]{1,0:T(8,128)(2,1)} %refs_5_.1, bf16[1024,8192]{1,0:T(8,128)(2,1)} %refs_6_.1, bf16[1024,512]{1,0:T(8,128)(2,1)} %refs_7_.1, ...), custom_call_target="tpu_custom_call" | custom-call | tf_op jit(solution)/shard_map/fused/pallas_call | solution.py:742
  53.3 1.5 %copy.16 = bf16[32,1024]{1,0:T(8,128)(2,1)} copy(bf16[32,1024]{1,0:T(8,128)(2,1)} %fused.1) | data formatting | bytes 131072

commit v7 on v6

--- a/solution.py
+++ b/solution.py
@@ -471,8 +471,14 @@
     blocks = 2 * SIDES
 
     def attend(h, between):
+        def part(b):
+            return 1 - core if b < SIDES else core
+
+        def base(b):
+            return (part(b) * SIDES + b % SIDES) * tq
+
         def query(b):
-            return r.gat[h, b // SIDES, b % SIDES].reshape(rows, HD)
+            return r.gat[h, part(b), b % SIDES].reshape(rows, HD)
 
         def self_kv(e):
             unit = 2 * h + e
@@ -494,12 +500,16 @@
 
         def small_scores(b, q):
             demo, bias = [], []
+            for t in range(0, tq, 2):
+                tok = base(b) + t
+                k = jnp.concatenate([r.dkb[h, r.tasks[tok + p]] for p in range(2)], axis=0)
+                s = nt(q[t * group : (t + 2) * group], k) * const
+                for p in range(2):
+                    x = s[p * group : (p + 1) * group, p * cfg.demo_dev : (p + 1) * cfg.demo_dev]
+                    demo.append(x + r.dmask[pl.ds(tok + p, 1), :])
             for t in range(tq):
-                tok = b * tq + t
-                k = r.dkb[h, r.tasks[tok]]
-                s = nt(q[t * group : (t + 1) * group], k) * const
-                demo.append(s + r.dmask[tok : tok + 1, :])
-                bias.append(jnp.broadcast_to(r.smask[tok : tok + 1, :], (group, qtok)))
+                tok = base(b) + t
+                bias.append(jnp.broadcast_to(r.smask[pl.ds(tok, 1), :], (group, qtok)))
             own = nt(q, self_k) * const + jnp.concatenate(bias, axis=0)
             return jnp.concatenate(demo, axis=0), own
 
@@ -511,15 +521,17 @@
             value = nn(r.wts[b % 2][...], r.pvb[h]) + nn(e.w_self, self_v)
             value = value + jnp.concatenate(
                 [
-                    nn(e.w_demo[t * group : (t + 1) * group], r.dvb[h, r.tasks[b * tq + t]])
+                    nn(e.w_demo[t * group : (t + 1) * group], r.dvb[h, r.tasks[base(b) + t]])
                     for t in range(tq)
                 ],
                 axis=0,
             )
             lane = lax.broadcasted_iota(jnp.int32, (rows, HD), 1)
-            c, n = b // SIDES, b % SIDES
+            c, n = part(b), b % SIDES
             r.pstat[h, c, n] = jnp.where(lane == 0, e.top, total).T[:STAT]
             r.pval[h, c, n] = value
+            if b == SIDES - 1:
+                start(send_pair(h))
 
         q = query(0)
         run = first()
@@ -559,7 +571,6 @@
             before = e
             between(b)
         finish(blocks - 1, before)
-        start(send_pair(h))
 
     def relay(h):
         pass_on(*o_gather(h), r.sh.at[h], r.rh.at[h])

time: 54.9 us -> 52.8 us (0.962)
  Pallas kernels: 53.2 us -> 51.2 us
    pallas_call x1, Pallas kernels: 53.2 us -> 51.2 us  [body(): pl.pallas_call(run, name='fused', out_shape=jax.ShapeDtypeStruct((qtok, c...]
where the time goes in v7:
time: 52.8 us; the launch traced here: 52.6 us
  Pallas kernels  51.2 us (97%)
  local copies, waits for them, and re-layouts  1.47 us (3%)
    pallas_call x1, Pallas kernels, body(): pl.pallas_call(run, name='fused', out_shape=jax.ShapeDtypeStruct((qtok, c...  51.2 us
    unnamed x1, local copies, waits for them, and re-layouts  1.47 us

profile of v7, /device:TPU:0, one launch (start us, length us, event | category | flops | bytes accessed | tf_op | source)
XLA Modules:
  0.0 52.6 jit_solution(3871971659139509987)
XLA Ops:
  0.0 51.2 %fused.1 = bf16[32,1024]{1,0:T(8,128)(2,1)} custom-call(s32[32]{0:T(128)} %refs_0_.1, s32[16]{0:T(128)} %refs_1_.1, s32[32]{0:T(128)} %refs_2_.1, f32[4,16]{1,0:T(4,128)} %bitcast.2, f32[4,16]{1,0:T(4,128)} %bitcast.3, bf16[32,1024]{1,0:T(8,128)(2,1)} %refs_5_.1, bf16[1024,8192]{1,0:T(8,128)(2,1)} %refs_6_.1, bf16[1024,512]{1,0:T(8,128)(2,1)} %refs_7_.1, ...), custom_call_target="tpu_custom_call" | custom-call | tf_op jit(solution)/shard_map/fused/pallas_call | solution.py:753
  51.2 1.5 %copy.16 = bf16[32,1024]{1,0:T(8,128)(2,1)} copy(bf16[32,1024]{1,0:T(8,128)(2,1)} %fused.1) | data formatting | bytes 131072
